TPU v7x, 32 devices: a whole 2x2x4 slice. The times are simulated.
32 devices in a mesh: dp: 4 (over x, core), fsdp: 8 (over z, y).
Axes of the slice: x: 2, y: 2, z: 4, core: 2. Of those that a mesh axis runs over, the one named last changes fastest.
Arguments:
- tokens: bfloat16 [8192, 1024], P(('dp', 'fsdp')), may hold values from -6 to 6
- patch_counts: int32 [32, 4], P(('dp', 'fsdp')), may hold values from 0 to 256, as said below
- norm_one_gain: bfloat16 [1024], P('fsdp'), may hold values from 0.25 to 1.75
- norm_one_shift: bfloat16 [1024], P('fsdp'), may hold values from -3 to 3
- joint_weight: bfloat16 [1024, 3072], P('fsdp'), may hold values from -0.1875 to 0.1875
- query_bias: bfloat16 [1024], P('fsdp'), may hold values from -3 to 3
- value_bias: bfloat16 [1024], P('fsdp'), may hold values from -3 to 3
- output_weight: bfloat16 [1024, 1024], P('fsdp'), may hold values from -1 to 1
- output_bias: bfloat16 [1024], P('fsdp'), may hold values from -3 to 3
- norm_two_gain: bfloat16 [1024], P('fsdp'), may hold values from 0.25 to 1.75
- norm_two_shift: bfloat16 [1024], P('fsdp'), may hold values from -3 to 3
- expand_weight: bfloat16 [1024, 4096], P('fsdp'), may hold values from -0.1875 to 0.1875
- expand_bias: bfloat16 [4096], P('fsdp'), may hold values from -3 to 3
- shrink_weight: bfloat16 [4096, 1024], P('fsdp'), may hold values from -0.09375 to 0.09375
- shrink_bias: bfloat16 [1024], P('fsdp'), may hold values from -3 to 3
- cotangent: bfloat16 [8192, 1024], P(('dp', 'fsdp')), may hold values from -6 to 6
Outputs:
- output: bfloat16 [8192, 1024], P(('dp', 'fsdp'))
- tokens_grad: bfloat16 [8192, 1024], P(('dp', 'fsdp'))
- grad_norm_one_gain: float32 [1024], P('fsdp')
- grad_norm_one_shift: float32 [1024], P('fsdp')
- grad_joint_weight: float32 [1024, 3072], P('fsdp')
- grad_query_bias: float32 [1024], P('fsdp')
- grad_value_bias: float32 [1024], P('fsdp')
- grad_output_weight: float32 [1024, 1024], P('fsdp')
- grad_output_bias: float32 [1024], P('fsdp')
- grad_norm_two_gain: float32 [1024], P('fsdp')
- grad_norm_two_shift: float32 [1024], P('fsdp')
- grad_expand_weight: float32 [1024, 4096], P('fsdp')
- grad_expand_bias: float32 [4096], P('fsdp')
- grad_shrink_weight: float32 [4096, 1024], P('fsdp')
- grad_shrink_bias: float32 [1024], P('fsdp')
Inputs may be any that keep to these rules, and one draw needn't show every extreme that they name: `patch_counts`: row d lists the patch counts of device d's images in its first slots, zeros after them. A device holds one image of 256 patches, or one or two of 128, or two to four of 64; each kind occurs on some device.
All inputs are finite; a program needn't handle non-finite values.
Results may differ from a plain program's by a relative error of at most 0.019.
Values may be sent and summed in bfloat16 or wider, within the bound.
A program may use at most 192 MiB of HBM per device.

v0:
```python
import jax
import jax.numpy as jnp
from jax import lax
from jax.sharding import PartitionSpec as P

HEADS = 16


epsilon = 1e-05
masked_score = -1e30


def norm_rows(values, gain, shift):
    centre = jnp.mean(values, axis=-1, keepdims=True)
    centred = values - centre
    spread = jnp.mean(centred * centred, axis=-1, keepdims=True)
    return centred * lax.rsqrt(spread + epsilon) * gain + shift


def image_rows(counts, length):
    ends = jnp.cumsum(counts[0])
    places = jnp.arange(length, dtype=jnp.int32)
    images = jnp.sum((places[:, None] >= ends[None, :]).astype(jnp.int32), axis=1)
    living = (places < ends[-1]).astype(jnp.float32)
    return (images, living)


def full_dot(left, right):
    return jnp.dot(left, right, preferred_element_type=jnp.float32)


def rows_dot(left, right):
    return lax.dot_general(
        left, right, (((0,), (0,)), ((), ())), preferred_element_type=jnp.float32
    )


def back_dot(left, right):
    return lax.dot_general(
        left, right, (((1,), (1,)), ((), ())), preferred_element_type=jnp.float32
    )


def column_sum(values):
    return jnp.sum(values, axis=0, dtype=jnp.float32)


def exact_gelu(values):
    return jax.nn.gelu(values, approximate=False)


def score_block(query_block, key_heads, image_block, images, scale):
    raw = (
        jnp.einsum("qhd,khd->hqk", query_block, key_heads, preferred_element_type=jnp.float32)
        * scale
    )
    same = image_block[:, None] == images[None, :]
    return jnp.where(same[None, :, :], raw, masked_score)


def attend_forward(queries, keys_all, values_all, images, block):
    length, width = queries.shape
    head_size = width // HEADS
    scale = head_size ** (-0.5)
    count = length // block
    query_blocks = queries.reshape(count, block, HEADS, head_size)
    key_heads = keys_all.reshape(length, HEADS, head_size)
    value_heads = values_all.reshape(length, HEADS, head_size)
    image_blocks = images.reshape(count, block)

    def one_block(bundle):
        query_block, image_block = bundle
        scores = score_block(query_block, key_heads, image_block, images, scale)
        top_score = jnp.max(scores, axis=-1, keepdims=True)
        exponent = jnp.exp(scores - top_score)
        total = jnp.sum(exponent, axis=-1, keepdims=True)
        weights = (exponent / total).astype(jnp.bfloat16)
        mixed = jnp.einsum("hqk,khd->qhd", weights, value_heads, preferred_element_type=jnp.float32)
        return (mixed.reshape(block, width), (top_score + jnp.log(total))[:, :, 0])

    mixed, log_total = lax.map(one_block, (query_blocks, image_blocks))
    return (mixed.reshape(length, width), log_total)


def attend_backward(queries, keys_all, values_all, images, log_total, mixed_grad, block):
    length, width = queries.shape
    head_size = width // HEADS
    scale = head_size ** (-0.5)
    count = length // block
    query_blocks = queries.reshape(count, block, HEADS, head_size)
    key_heads = keys_all.reshape(length, HEADS, head_size)
    value_heads = values_all.reshape(length, HEADS, head_size)
    image_blocks = images.reshape(count, block)
    grad_blocks = mixed_grad.reshape(count, block, HEADS, head_size)

    def one_block(carry, bundle):
        key_acc, value_acc = carry
        query_block, image_block, total_block, grad_block = bundle
        scores = score_block(query_block, key_heads, image_block, images, scale)
        weights = jnp.exp(scores - total_block[:, :, None])
        weight_grad = jnp.einsum(
            "qhd,khd->hqk", grad_block, value_heads, preferred_element_type=jnp.float32
        )
        inner = jnp.sum(weights * weight_grad, axis=-1, keepdims=True)
        score_grad = (weights * (weight_grad - inner)).astype(jnp.bfloat16)
        query_part = (
            jnp.einsum("hqk,khd->qhd", score_grad, key_heads, preferred_element_type=jnp.float32)
            * scale
        )
        key_acc = (
            key_acc
            + jnp.einsum(
                "hqk,qhd->khd", score_grad, query_block, preferred_element_type=jnp.float32
            )
            * scale
        )
        value_acc = value_acc + jnp.einsum(
            "hqk,qhd->khd",
            weights.astype(jnp.bfloat16),
            grad_block,
            preferred_element_type=jnp.float32,
        )
        return ((key_acc, value_acc), query_part)

    zeros = jnp.zeros((length, HEADS, head_size), jnp.float32)
    (key_grad, value_grad), query_grad = lax.scan(
        one_block, (zeros, zeros), (query_blocks, image_blocks, log_total, grad_blocks)
    )
    return (
        query_grad.reshape(length, width),
        key_grad.reshape(length, width),
        value_grad.reshape(length, width),
    )


def forward(x_float, images, living, attn_full, mlp_full, block):
    gain_one, shift_one, joint_w, query_b, value_b, out_w, out_b = attn_full
    gain_two, shift_two, expand_w, expand_b, shrink_w, shrink_b = mlp_full
    width = x_float.shape[1]
    normed_one = norm_rows(x_float, gain_one, shift_one).astype(jnp.bfloat16)
    joint = full_dot(normed_one, joint_w)
    queries = (joint[:, :width] + query_b).astype(jnp.bfloat16)
    keys_all = joint[:, width : 2 * width].astype(jnp.bfloat16)
    values_all = (joint[:, 2 * width :] + value_b).astype(jnp.bfloat16)
    mixed, log_total = attend_forward(queries, keys_all, values_all, images, block)
    mixed = mixed.astype(jnp.bfloat16)
    first = x_float + (full_dot(mixed, out_w) + out_b)
    normed_two = norm_rows(first, gain_two, shift_two).astype(jnp.bfloat16)
    hidden_pre = full_dot(normed_two, expand_w) + expand_b
    hidden_act = exact_gelu(hidden_pre).astype(jnp.bfloat16)
    result = (first + full_dot(hidden_act, shrink_w) + shrink_b) * living[:, None]
    saved = (
        normed_one,
        queries,
        keys_all,
        values_all,
        log_total,
        mixed,
        first,
        normed_two,
        hidden_pre,
        hidden_act,
    )
    return (result, saved)


def body(
    tokens,
    patch_counts,
    norm_one_gain,
    norm_one_shift,
    joint_weight,
    query_bias,
    value_bias,
    output_weight,
    output_bias,
    norm_two_gain,
    norm_two_shift,
    expand_weight,
    expand_bias,
    shrink_weight,
    shrink_bias,
    cotangent,
):
    length = tokens.shape[0]
    block = min(length, 512)
    images, living = image_rows(patch_counts, length)
    x_float = tokens.astype(jnp.float32)
    attn_full = (
        lax.all_gather(norm_one_gain, "fsdp", axis=0, tiled=True),
        lax.all_gather(norm_one_shift, "fsdp", axis=0, tiled=True),
        lax.all_gather(joint_weight, "fsdp", axis=0, tiled=True),
        lax.all_gather(query_bias, "fsdp", axis=0, tiled=True),
        lax.all_gather(value_bias, "fsdp", axis=0, tiled=True),
        lax.all_gather(output_weight, "fsdp", axis=0, tiled=True),
        lax.all_gather(output_bias, "fsdp", axis=0, tiled=True),
    )
    mlp_full = (
        lax.all_gather(norm_two_gain, "fsdp", axis=0, tiled=True),
        lax.all_gather(norm_two_shift, "fsdp", axis=0, tiled=True),
        lax.all_gather(expand_weight, "fsdp", axis=0, tiled=True),
        lax.all_gather(expand_bias, "fsdp", axis=0, tiled=True),
        lax.all_gather(shrink_weight, "fsdp", axis=0, tiled=True),
        lax.all_gather(shrink_bias, "fsdp", axis=0, tiled=True),
    )
    result, saved = forward(x_float, images, living, attn_full, mlp_full, block)
    attn_used = (
        lax.all_gather(norm_one_gain, "fsdp", axis=0, tiled=True),
        lax.all_gather(norm_one_shift, "fsdp", axis=0, tiled=True),
        lax.all_gather(joint_weight, "fsdp", axis=0, tiled=True),
        lax.all_gather(query_bias, "fsdp", axis=0, tiled=True),
        lax.all_gather(value_bias, "fsdp", axis=0, tiled=True),
        lax.all_gather(output_weight, "fsdp", axis=0, tiled=True),
        lax.all_gather(output_bias, "fsdp", axis=0, tiled=True),
    )
    mlp_used = (
        lax.all_gather(norm_two_gain, "fsdp", axis=0, tiled=True),
        lax.all_gather(norm_two_shift, "fsdp", axis=0, tiled=True),
        lax.all_gather(expand_weight, "fsdp", axis=0, tiled=True),
        lax.all_gather(expand_bias, "fsdp", axis=0, tiled=True),
        lax.all_gather(shrink_weight, "fsdp", axis=0, tiled=True),
        lax.all_gather(shrink_bias, "fsdp", axis=0, tiled=True),
    )
    unused_result, saved = forward(x_float, images, living, attn_used, mlp_used, block)
    gain_one, shift_one, joint_w, query_b, value_b, out_w, out_b = attn_used
    gain_two, shift_two, expand_w, expand_b, shrink_w, shrink_b = mlp_used
    (
        normed_one,
        queries,
        keys_all,
        values_all,
        log_total,
        mixed,
        first,
        normed_two,
        hidden_pre,
        hidden_act,
    ) = saved
    out_grad = cotangent.astype(jnp.float32) * living[:, None]
    branch_grad = out_grad.astype(jnp.bfloat16)
    shrink_bias_term = column_sum(branch_grad)
    shrink_weight_term = rows_dot(hidden_act, branch_grad)
    act_grad = back_dot(branch_grad, shrink_w)
    unused_act, gelu_pull = jax.vjp(exact_gelu, hidden_pre)
    hidden_grad = gelu_pull(act_grad)[0].astype(jnp.bfloat16)
    expand_bias_term = column_sum(hidden_grad)
    expand_weight_term = rows_dot(normed_two, hidden_grad)
    two_grad = back_dot(hidden_grad, expand_w)
    unused_two, norm_two_pull = jax.vjp(
        norm_rows, first, gain_two.astype(jnp.float32), shift_two.astype(jnp.float32)
    )
    first_part, gain_two_term, shift_two_term = norm_two_pull(two_grad)
    mlp_terms = (
        gain_two_term,
        shift_two_term,
        expand_weight_term,
        expand_bias_term,
        shrink_weight_term,
        shrink_bias_term,
    )
    mlp_shards = (
        lax.psum_scatter(
            mlp_terms[0].astype(jnp.bfloat16), "fsdp", scatter_dimension=0, tiled=True
        ).astype(jnp.float32),
        lax.psum_scatter(
            mlp_terms[1].astype(jnp.bfloat16), "fsdp", scatter_dimension=0, tiled=True
        ).astype(jnp.float32),
        lax.psum_scatter(
            mlp_terms[2].astype(jnp.bfloat16), "fsdp", scatter_dimension=0, tiled=True
        ).astype(jnp.float32),
        lax.psum_scatter(
            mlp_terms[3].astype(jnp.bfloat16), "fsdp", scatter_dimension=0, tiled=True
        ).astype(jnp.float32),
        lax.psum_scatter(
            mlp_terms[4].astype(jnp.bfloat16), "fsdp", scatter_dimension=0, tiled=True
        ).astype(jnp.float32),
        lax.psum_scatter(
            mlp_terms[5].astype(jnp.bfloat16), "fsdp", scatter_dimension=0, tiled=True
        ).astype(jnp.float32),
    )
    first_grad = out_grad + first_part
    proj_grad = first_grad.astype(jnp.bfloat16)
    out_bias_term = column_sum(proj_grad)
    out_weight_term = rows_dot(mixed, proj_grad)
    mixed_grad = back_dot(proj_grad, out_w).astype(jnp.bfloat16)
    query_grad, key_grad, value_grad = attend_backward(
        queries, keys_all, values_all, images, log_total, mixed_grad, block
    )
    query_grad = query_grad.astype(jnp.bfloat16)
    key_grad = key_grad.astype(jnp.bfloat16)
    value_grad = value_grad.astype(jnp.bfloat16)
    query_bias_term = column_sum(query_grad)
    value_bias_term = column_sum(value_grad)
    joint_grad = jnp.concatenate([query_grad, key_grad, value_grad], axis=1)
    joint_weight_term = rows_dot(normed_one, joint_grad)
    one_grad = back_dot(joint_grad, joint_w)
    unused_one, norm_one_pull = jax.vjp(
        norm_rows, x_float, gain_one.astype(jnp.float32), shift_one.astype(jnp.float32)
    )
    input_part, gain_one_term, shift_one_term = norm_one_pull(one_grad)
    tokens_grad = (first_grad + input_part).astype(jnp.bfloat16)
    attn_shards = (
        lax.psum_scatter(
            gain_one_term.astype(jnp.bfloat16), "fsdp", scatter_dimension=0, tiled=True
        ).astype(jnp.float32),
        lax.psum_scatter(
            shift_one_term.astype(jnp.bfloat16), "fsdp", scatter_dimension=0, tiled=True
        ).astype(jnp.float32),
        lax.psum_scatter(
            joint_weight_term.astype(jnp.bfloat16), "fsdp", scatter_dimension=0, tiled=True
        ).astype(jnp.float32),
        lax.psum_scatter(
            query_bias_term.astype(jnp.bfloat16), "fsdp", scatter_dimension=0, tiled=True
        ).astype(jnp.float32),
        lax.psum_scatter(
            value_bias_term.astype(jnp.bfloat16), "fsdp", scatter_dimension=0, tiled=True
        ).astype(jnp.float32),
        lax.psum_scatter(
            out_weight_term.astype(jnp.bfloat16), "fsdp", scatter_dimension=0, tiled=True
        ).astype(jnp.float32),
        lax.psum_scatter(
            out_bias_term.astype(jnp.bfloat16), "fsdp", scatter_dimension=0, tiled=True
        ).astype(jnp.float32),
    )
    summed = (
        lax.psum(attn_shards[0].astype(jnp.bfloat16), "dp").astype(jnp.float32),
        lax.psum(attn_shards[1].astype(jnp.bfloat16), "dp").astype(jnp.float32),
        lax.psum(attn_shards[2].astype(jnp.bfloat16), "dp").astype(jnp.float32),
        lax.psum(attn_shards[3].astype(jnp.bfloat16), "dp").astype(jnp.float32),
        lax.psum(attn_shards[4].astype(jnp.bfloat16), "dp").astype(jnp.float32),
        lax.psum(attn_shards[5].astype(jnp.bfloat16), "dp").astype(jnp.float32),
        lax.psum(attn_shards[6].astype(jnp.bfloat16), "dp").astype(jnp.float32),
        lax.psum(mlp_shards[0].astype(jnp.bfloat16), "dp").astype(jnp.float32),
        lax.psum(mlp_shards[1].astype(jnp.bfloat16), "dp").astype(jnp.float32),
        lax.psum(mlp_shards[2].astype(jnp.bfloat16), "dp").astype(jnp.float32),
        lax.psum(mlp_shards[3].astype(jnp.bfloat16), "dp").astype(jnp.float32),
        lax.psum(mlp_shards[4].astype(jnp.bfloat16), "dp").astype(jnp.float32),
        lax.psum(mlp_shards[5].astype(jnp.bfloat16), "dp").astype(jnp.float32),
    )
    divisor = float(lax.axis_size("dp") * lax.axis_size("fsdp"))
    means = tuple((total / divisor for total in summed))
    return (
        result.astype(jnp.bfloat16),
        tokens_grad,
        means[0],
        means[1],
        means[2],
        means[3],
        means[4],
        means[5],
        means[6],
        means[7],
        means[8],
        means[9],
        means[10],
        means[11],
        means[12],
    )


def solution(mesh):
    in_specs = (
        P(("dp", "fsdp"), None),
        P(("dp", "fsdp"), None),
        P("fsdp"),
        P("fsdp"),
        P("fsdp", None),
        P("fsdp"),
        P("fsdp"),
        P("fsdp", None),
        P("fsdp"),
        P("fsdp"),
        P("fsdp"),
        P("fsdp", None),
        P("fsdp"),
        P("fsdp", None),
        P("fsdp"),
        P(("dp", "fsdp"), None),
    )
    out_specs = (
        P(("dp", "fsdp"), None),
        P(("dp", "fsdp"), None),
        P("fsdp"),
        P("fsdp"),
        P("fsdp", None),
        P("fsdp"),
        P("fsdp"),
        P("fsdp", None),
        P("fsdp"),
        P("fsdp"),
        P("fsdp"),
        P("fsdp", None),
        P("fsdp"),
        P("fsdp", None),
        P("fsdp"),
    )
    return jax.shard_map(body, mesh=mesh, in_specs=in_specs, out_specs=out_specs, check_vma=False)
```

profile of v0, /device:TPU:3, one launch (start us, length us, event | category | flops | bytes accessed | tf_op | source)
XLA Modules:
  0.0 1001.3 jit_solution(14271259691791747192)
XLA Ops:
  12.1 17.5 %all-gather = bf16[8,1,128]{2,1,0:T(2,128)(2,1)S(1)} all-gather(bf16[1,1,128]{2,1,0:T(2,128)(2,1)} %bitcast.97), channel_id=1, replica_groups=mesh['dp'=4,'fsdp'=8] {'fsdp'}, dimensions={0}, use_global_device_ids=true | all-gather | bytes 2304 | tf_op jit(solution)/shard_map/all_gather | solution.py:190
  29.6 13.6 %all-gather.1 = bf16[8,1,128]{2,1,0:T(2,128)(2,1)S(1)} all-gather(bf16[1,1,128]{2,1,0:T(2,128)(2,1)} %bitcast.98), channel_id=1, replica_groups=mesh['dp'=4,'fsdp'=8] {'fsdp'}, dimensions={0}, use_global_device_ids=true | all-gather | bytes 2304 | tf_op jit(solution)/shard_map/all_gather | solution.py:191
  43.2 14.9 %all-gather.3 = bf16[8,1,128]{2,1,0:T(2,128)(2,1)S(1)} all-gather(bf16[1,1,128]{2,1,0:T(2,128)(2,1)} %bitcast.99), channel_id=1, replica_groups=mesh['dp'=4,'fsdp'=8] {'fsdp'}, dimensions={0}, use_global_device_ids=true | all-gather | bytes 2304 | tf_op jit(solution)/shard_map/all_gather | solution.py:193
  58.2 13.9 %all-gather.2 = bf16[8,1,128]{2,1,0:T(2,128)(2,1)S(1)} all-gather(bf16[1,1,128]{2,1,0:T(2,128)(2,1)} %bitcast.100), channel_id=1, replica_groups=mesh['dp'=4,'fsdp'=8] {'fsdp'}, dimensions={0}, use_global_device_ids=true | all-gather | bytes 2304 | tf_op jit(solution)/shard_map/all_gather | solution.py:194
  72.1 16.2 %all-gather.4 = bf16[8,1,128]{2,1,0:T(2,128)(2,1)S(1)} all-gather(bf16[1,1,128]{2,1,0:T(2,128)(2,1)} %bitcast.101), channel_id=1, replica_groups=mesh['dp'=4,'fsdp'=8] {'fsdp'}, dimensions={0}, use_global_device_ids=true | all-gather | bytes 2304 | tf_op jit(solution)/shard_map/all_gather | solution.py:196
  88.3 13.3 %all-gather.5 = bf16[8,1,128]{2,1,0:T(2,128)(2,1)S(1)} all-gather(bf16[1,1,128]{2,1,0:T(2,128)(2,1)} %bitcast.102), channel_id=1, replica_groups=mesh['dp'=4,'fsdp'=8] {'fsdp'}, dimensions={0}, use_global_device_ids=true | all-gather | bytes 2304 | tf_op jit(solution)/shard_map/all_gather | solution.py:199
  101.6 15.2 %all-gather.6 = bf16[8,1,128]{2,1,0:T(2,128)(2,1)S(1)} all-gather(bf16[1,1,128]{2,1,0:T(2,128)(2,1)} %bitcast.103), channel_id=1, replica_groups=mesh['dp'=4,'fsdp'=8] {'fsdp'}, dimensions={0}, use_global_device_ids=true | all-gather | bytes 2304 | tf_op jit(solution)/shard_map/all_gather | solution.py:200
  116.9 22.4 %all-gather.7 = bf16[8,1,512]{2,1,0:T(2,128)(2,1)S(1)} all-gather(bf16[1,1,512]{2,1,0:T(2,128)(2,1)S(1)} %reshape.213), channel_id=1, replica_groups=mesh['dp'=4,'fsdp'=8] {'fsdp'}, dimensions={0}, use_global_device_ids=true | all-gather | bytes 9216 | tf_op jit(solution)/shard_map/all_gather | solution.py:202
  151.1 7.1 all-gather.16.cloned.1.call-done
  160.9 123.8 %all-gather.18.cloned.1.call-done = bf16[1024,4096]{1,0:T(8,128)(2,1)} async-done(((bf16[128,4096]{1,0:T(8,128)(2,1)}), bf16[1024,4096]{1,0:T(8,128)(2,1)}) %all-gather.18.cloned.1.call-update) | async-done | bytes 8388624 | tf_op jit(solution)/shard_map/all_gather | solution.py:201
  284.7 16.2 %multiply_convert_fusion.1 = (bf16[256,4096]{1,0:T(8,128)(2,1)}, f32[256,4096]{1,0:T(8,128)}, f32[256,4096]{1,0:T(8,128)}) fusion(f32[4096]{0:T(1024)S(1)} %bitcast.93, bf16[1024,4096]{1,0:T(8,128)(2,1)} %all-gather.18.cloned.1.call-done, f32[256,1024]{1,0:T(8,128)S(1)} %get-tuple-element.134, f32[1024]{0:T(1024)S(1)} %bitcast.83, f32[1024]{0:T(1024)S(1)} %bitcast.79, ...), kind=kOutput, calls=%fused_computation.10 | convolution fusion | flops 2218000384 | bytes 19949568 | tf_op jit(solution)/shard_map/dot_general | solution.py:29
  300.9 108.5 %all-gather.20.cloned.1.call-done = bf16[4096,1024]{1,0:T(8,128)(2,1)} async-done(((bf16[512,1024]{1,0:T(8,128)(2,1)}), bf16[4096,1024]{1,0:T(8,128)(2,1)}) %all-gather.20.cloned.1.call-update) | async-done | bytes 8388624 | tf_op jit(solution)/shard_map/all_gather | solution.py:203
  409.4 11.8 %fusion.60 = (bf16[4096]{0:T(1024)(128)(2,1)S(1)}, bf16[256,4096]{1,0:T(8,128)(2,1)S(1)}) fusion(f32[256,4096]{1,0:T(8,128)} %get-tuple-element.127, f32[256,4096]{1,0:T(8,128)} %get-tuple-element.135, bf16[4096,1024]{1,0:T(8,128)(2,1)} %all-gather.20.cloned.1.call-done, bf16[256,1024]{1,0:T(8,128)(2,1)S(1)} %copy-done.7, f32[256]{0:T(256)S(1)} %compare_convert_fusion), kind=kOutput, calls=%fused_computation.118 | convolution fusion | flops 2163994624 | bytes 19407872 | tf_op jit(solution)/shard_map/dot_general | solution.py:39
  445.1 7.4 convolution_convert_fusion.1
  453.5 7.3 convolution_convert_fusion
  463.4 14.6 %all-gather.8 = bf16[8,1,128]{2,1,0:T(2,128)(2,1)S(1)} all-gather(bf16[1,1,128]{2,1,0:T(2,128)(2,1)S(1)} %bitcast.104), channel_id=1, replica_groups=mesh['dp'=4,'fsdp'=8] {'fsdp'}, dimensions={0}, use_global_device_ids=true | all-gather | bytes 2304 | tf_op jit(solution)/shard_map/all_gather | solution.py:204
  478.1 5.4 fusion.51
  485.1 26.6 %all-reduce.9 = (bf16[1024]{0:T(1024)(128)(2,1)S(1)}, bf16[1024]{0:T(1024)(128)(2,1)S(1)}, bf16[1024]{0:T(1024)(128)(2,1)S(1)}, bf16[1024]{0:T(1024)(128)(2,1)S(...) all-reduce(bf16[1024]{0:T(1024)(128)(2,1)S(1)} %get-tuple-element.8, ...), channel_id=2, replica_groups=mesh['dp'=4,'fsdp'=8] {'fsdp'}, use_global_device_ids=true, to_apply=%region_14.15.clone | all-reduce | flops 12288 | bytes 49152
  512.3 17.3 %all-reduce.10 = (bf16[128]{0:T(256)(128)(2,1)S(1)}, bf16[128]{0:T(256)(128)(2,1)S(1)}, bf16[128]{0:T(256)(128)(2,1)S(1)}, bf16[128]{0:T(256)(128)(2,1)S(1)}, bf...) all-reduce(bf16[128]{0:T(256)(128)(2,1)S(1)} %dynamic-slice.2, ...), channel_id=1, replica_groups=mesh['dp'=4,'fsdp'=8] {'dp'}, use_global_device_ids=true, to_apply=%region_15.16 | all-reduce | flops 1536 | bytes 6144 | tf_op jit(solution)/shard_map/psum | solution.py:326
  531.2 83.7 %reduce-scatter.5.cloned.1.call-done = bf16[128,3072]{1,0:T(8,128)(2,1)} async-done(((bf16[1024,3072]{1,0:T(8,128)(2,1)}), bf16[128,3072]{1,0:T(8,128)(2,1)}) %reduce-scatter.5.cloned.1.call-update) | async-done | bytes 786448 | tf_op jit(solution)/shard_map/reduce_scatter | solution.py:309
  614.9 150.9 %reduce-scatter.9.cloned.1.call-done = bf16[128,4096]{1,0:T(8,128)(2,1)} async-done(((bf16[1024,4096]{1,0:T(8,128)(2,1)}), bf16[128,4096]{1,0:T(8,128)(2,1)}) %reduce-scatter.9.cloned.1.call-update) | async-done | bytes 1048592 | tf_op jit(solution)/shard_map/reduce_scatter | solution.py:268
  765.7 150.2 %reduce-scatter.11.cloned.1.call-done = bf16[512,1024]{1,0:T(8,128)(2,1)} async-done(((bf16[4096,1024]{1,0:T(8,128)(2,1)}), bf16[512,1024]{1,0:T(8,128)(2,1)}) %reduce-scatter.11.cloned.1.call-update) | async-done | bytes 1048592 | tf_op jit(solution)/shard_map/reduce_scatter | solution.py:274
  919.6 7.2 fusion.18
  926.8 58.8 %all-reduce.14.cloned.1.call-done = (bf16[128,3072]{1,0:T(8,128)(2,1)}, bf16[128,1024]{1,0:T(8,128)(2,1)}, bf16[128,4096]{1,0:T(8,128)(2,1)}, bf16[512,1024]{1,0:T(8,128)(2,1)}) async-done(((bf16[128,3072]{1,0:T(8,128)(2,1)}, bf16[128,1024]{1,0:T(8,128)(2,1)}, bf16[128,4096]{1,0:T(8,128)(2,1)}, bf16[512,1024]{1,0:T(8,128)(2,1)}), (bf16[128,3072]{1,0:T(8,128)(2,1)}, bf16[128,1024]{1,0:T(8,128)(2,1)}, ...) | async-done | bytes 3145744 | tf_op jit(solution)/shard_map/psum | solution.py:328
  (136 shorter events, 61.5 us)
Async XLA Ops:
  7.2 134.1 %copy-start.2 = (bf16[256,1024]{1,0:T(8,128)(2,1)S(1)}, bf16[256,1024]{1,0:T(8,128)(2,1)}, u32[]{:S(2)}) copy-start(bf16[256,1024]{1,0:T(8,128)(2,1)} %param.16) | copy-start | bytes 1572868
  7.2 134.5 %all-gather.14.cloned.1.call-start = ((), (), s32[]{:S(2)}) async-start(), calls=%async_computation.4 | async-start | bytes 7077888 | tf_op jit(solution)/shard_map/all_gather | solution.py:192
  7.9 150.3 %all-gather.16.cloned.1.call-start = ((), (), s32[]{:S(2)}) async-start(), calls=%async_computation.5 | async-start | bytes 2359296 | tf_op jit(solution)/shard_map/all_gather | solution.py:195
  8.7 276.1 %all-gather.18.cloned.1.call-start = ((), (), s32[]{:S(2)}) async-start(), calls=%async_computation.6 | async-start | bytes 9437184 | tf_op jit(solution)/shard_map/all_gather | solution.py:201
  9.4 400.0 %all-gather.20.cloned.1.call-start = ((), (), s32[]{:S(2)}) async-start(), calls=%async_computation.7 | async-start | bytes 9437184 | tf_op jit(solution)/shard_map/all_gather | solution.py:203
  10.0 521.2 %reduce-scatter.7.cloned.1.call-start = ((), (), s32[]{:S(2)}) async-start(), calls=%async_computation.9 | async-start | bytes 2359296 | tf_op jit(solution)/shard_map/reduce_scatter | solution.py:318
  147.0 1.9 copy-start.5
  147.2 1.7 copy-start.3
  147.4 1.5 copy-start.11
  148.3 1.9 copy-start
  151.1 149.9 %copy-start.12 = (bf16[16,64,256]{2,1,0:T(8,128)(2,1)}, bf16[16,64,256]{2,1,0:T(8,128)(2,1)S(1)}, u32[]{:S(2)}) copy-start(bf16[16,64,256]{2,1,0:T(8,128)(2,1)S(1)} %fusion.24) | copy-start | bytes 1572868
  284.7 124.7 %copy-start.7 = (bf16[256,1024]{1,0:T(8,128)(2,1)S(1)}, bf16[256,1024]{1,0:T(8,128)(2,1)}, u32[]{:S(2)}) copy-start(bf16[256,1024]{1,0:T(8,128)(2,1)} %param.31) | copy-start | bytes 1572868
  409.4 11.8 %copy-start.20 = (bf16[1024,4096]{1,0:T(8,128)(2,1)S(1)}, bf16[1024,4096]{1,0:T(8,128)(2,1)}, u32[]{:S(2)}) copy-start(bf16[1024,4096]{1,0:T(8,128)(2,1)} %all-gather.18.cloned.1.call-done) | copy-start | bytes 25165828
  421.2 2.7 copy-start.10
  423.9 1.5 copy-start.13
  427.5 187.4 %reduce-scatter.5.cloned.1.call-start = ((), (), s32[]{:S(2)}) async-start(), calls=%async_computation.8 | async-start | bytes 7077888 | tf_op jit(solution)/shard_map/reduce_scatter | solution.py:309
  432.1 3.8 copy-start.1
  435.9 1.8 copy-start.4
  437.7 1.5 copy-start.17
  444.8 320.9 %reduce-scatter.9.cloned.1.call-start = ((), (), s32[]{:S(2)}) async-start(), calls=%async_computation.10 | async-start | bytes 9437184 | tf_op jit(solution)/shard_map/reduce_scatter | solution.py:268
  452.5 463.4 %reduce-scatter.11.cloned.1.call-start = ((), (), s32[]{:S(2)}) async-start(), calls=%async_computation.11 | async-start | bytes 9437184 | tf_op jit(solution)/shard_map/reduce_scatter | solution.py:274
  460.8 2.5 copy-start.19
  460.9 524.8 %all-reduce.14.cloned.1.call-start = ((), (), s32[]{:S(2)}) async-start(), calls=%async_computation.12 | async-start | bytes 6291456 | tf_op jit(solution)/shard_map/psum | solution.py:328
  985.6 7.1 copy-start.15
  (7 other events, 6.2 us)
Sparse Core Ops, SparseCore 0:
  10.2 98.8 all-gather.13
  111.2 46.9 all-gather.15
  160.4 124.3 all-gather.17
  286.7 122.6 all-gather.19
  427.6 65.7 reduce-scatter.6
  496.9 117.9 reduce-scatter.4
  618.5 147.2 reduce-scatter.8
  769.4 146.5 reduce-scatter.10
  918.5 67.0 all-reduce.13
where the time goes:
time: 1010 us; the launch traced here: 1000 us
  waiting for transfers between devices  686 us (68%)
  blocking collectives  186 us (18%)
  matrix products  82.7 us (8%)
  other arithmetic  20.5 us (2%)
  between operations  16 us (2%)
  local copies, waits for them, and re-layouts  10.2 us (1%)
    reduce_scatter x1, waiting for transfers between devices, body(): lax.psum_scatter(mlp_terms[2].astype(jnp.bfloat16), 'fsdp', scatter_dimen...  151 us
    reduce_scatter x1, waiting for transfers between devices, body(): lax.psum_scatter(mlp_terms[4].astype(jnp.bfloat16), 'fsdp', scatter_dimen...  150 us
    all_gather x1, waiting for transfers between devices, body(): lax.all_gather(expand_weight, 'fsdp', axis=0, tiled=True)  124 us
    all_gather x1, waiting for transfers between devices, body(): lax.all_gather(shrink_weight, 'fsdp', axis=0, tiled=True)  108 us
    reduce_scatter x1, waiting for transfers between devices, body(): lax.psum_scatter(joint_weight_term.astype(jnp.bfloat16), 'fsdp', scatter_...  83.7 us
    psum x1, waiting for transfers between devices, body(): lax.psum(attn_shards[2].astype(jnp.bfloat16), 'dp').astype(jnp.float32)  58.8 us
    dot_general x4, matrix products, full_dot(): return jnp.dot(left, right, preferred_element_type=jnp.float32)  30.5 us
    unnamed x1, blocking collectives  26.6 us
  transfers between devices with their start and end apart: 9, of which 7 were waited for; matrix products, arithmetic and copies ran while one was open for 8% of the time, Pallas kernels for 0%

commit v1 on v0

v1 whole, which is shorter than its diff:
```python
import functools
from types import SimpleNamespace

import jax
import jax.numpy as jnp
from jax import lax
from jax.experimental import pallas as pl
from jax.experimental.pallas import tpu as pltpu
from jax.sharding import PartitionSpec as P

HEADS = 16
EPS = 1e-05
MASKED = -1e30
MESH = pl.DeviceIdType.MESH
BF = jnp.bfloat16
F32 = jnp.float32
VROWS = 16
J, O, E, S, VEC = range(5)


class Sizes:
    def __init__(self, n_dp, n_fsdp, rows, width, hidden, slots):
        self.n_dp, self.n = n_dp, n_fsdp
        self.R, self.D, self.FF, self.slots = rows, width, hidden, slots
        self.Y = 2 ** ((n_fsdp.bit_length() - 1) // 2)
        self.Z = n_fsdp // self.Y
        T = 4 if n_dp % 4 == 0 else 2
        while hidden // n_fsdp // T % 128 or self.Z % T:
            T //= 2
        self.T, self.X = T, T // 2
        self.RT = T * rows
        self.Dn = width // n_fsdp
        self.DT = width // T
        self.H = HEADS // T
        self.hd = width // HEADS
        self.F = hidden // T
        self.FB = hidden // n_fsdp // T
        self.ZT = self.Z // T


def dot_nn(a, b):
    return jnp.dot(a, b, preferred_element_type=F32)


def dot_nt(a, b):
    return lax.dot_general(a, b, (((1,), (1,)), ((), ())), preferred_element_type=F32)


def dot_tn(a, b):
    return lax.dot_general(a, b, (((0,), (0,)), ((), ())), preferred_element_type=F32)


def ds(start, size, mult):
    return pl.ds(pl.multiple_of(start, mult), size)


def norm_parts(x):
    mean = jnp.mean(x, axis=-1, keepdims=True)
    xc = x - mean
    var = jnp.mean(xc * xc, axis=-1, keepdims=True)
    s = lax.rsqrt(var + EPS)
    return xc * s, s


def layout(q):
    R, D, T, RT = q.R, q.D, q.T, q.RT
    Cj = 3 * q.DT
    DMA = pltpu.SemaphoreType.DMA
    V = pltpu.VMEM
    m = SimpleNamespace()
    m.tok = V((T, R, D), BF)
    m.n1 = V((RT, D), BF)
    m.cot = V((T, R, D), BF)
    m.w = [V((D, Cj), BF), V((q.DT, D), BF), V((D, q.F), BF), V((q.F, D), BF)]
    m.qkv = V((RT, Cj), BF)
    m.prob = V((T * q.H, R, R), BF)
    m.mixed = V((RT, q.DT), BF)
    m.first = V((R, D), F32)
    m.n2 = V((T, R, D), BF)
    m.hact = V((RT, q.F), BF)
    m.dgelu = V((RT, q.F), BF)
    m.hgrad = V((RT, q.F), BF)
    m.proj = V((T, R, D), BF)
    m.fgrad = V((R, D), F32)
    m.mgrad = V((RT, q.DT), BF)
    m.jgrad = V((RT, Cj), BF)
    m.obuf = V((R, D), BF)
    m.tbuf = V((R, D), BF)
    m.acc0 = V((R, D), F32)
    m.psend = [V((q.X, R, D), BF) for _ in range(2)]
    m.precv = [V((q.X, R, D), BF) for _ in range(2)]
    m.xsend = [V((R, D) if q.X == 2 else (16, 128), BF) for _ in range(2)]
    m.xrecv = [V((R, D) if q.X == 2 else (16, 128), BF) for _ in range(2)]
    m.rs = [[DMA((q.X,)), DMA((q.X,)), DMA((1,)), DMA((1,))] for _ in range(4)]
    m.dw = [V((bz, q.Y * rb, C), BF) for bz, rb, C in q.grads]
    m.yr = [V((q.Y - 1, bz, rb, C), BF) for bz, rb, C in q.grads]
    m.zr = [V((q.Z - 1, rb, C), BF) for bz, rb, C in q.grads]
    m.fin = [V((1 if w == O else T, rb, C), BF) for w, (bz, rb, C) in enumerate(q.grads)]
    m.sy = [[DMA((q.Y - 1, bz)), DMA((q.Y - 1, bz))] for bz, rb, C in q.grads]
    m.sz = [[DMA((q.Z - 1,)), DMA((q.Z - 1,))] for _ in q.grads]
    m.sout = [DMA((T, q.n)) for _ in q.grads]
    m.gz = [[DMA((q.Z - 1,)), DMA((max(q.Z - 1, q.ZT),))] for _ in range(5)]
    m.gy = [[DMA((q.Y - 1, q.Z)), DMA((q.Y - 1, q.Z))] for _ in range(5)]
    pair = lambda: [DMA((3,)), DMA((3,))]
    m.ttok, m.tcot, m.tn2, m.tproj, m.tcnt, m.tfo = (pair() for _ in range(6))
    m.tfin = [pair() for _ in q.grads]
    m.vec = V((q.n, VROWS, q.Dn), BF)
    m.vf = V((8, D), F32)
    m.hb = V((8, q.F), F32)
    m.cnt = V((T, 8, 128), jnp.int32)
    m.vg = V((8, D), F32)
    m.vgh = V((8, q.F), F32)
    m.v3 = V((q.n, VROWS, q.Dn), F32)
    m.v3c = V((2, q.n, VROWS, q.Dn), F32)
    m.v3y = V((q.Y - 1, q.Z, VROWS, q.Dn), F32)
    m.v3s = V((q.Z, VROWS, q.Dn), F32)
    m.v3z = V((q.Z - 1, VROWS, q.Dn), F32)
    m.vout = V((VROWS, q.Dn), F32)
    m.svt = [DMA((2,)), DMA((2,))]
    m.svy = [DMA((q.Y - 1, q.Z)), DMA((q.Y - 1, q.Z))]
    m.svz = [DMA((q.Z - 1,)), DMA((q.Z - 1,))]
    m.loc = DMA((7 + q.n,))
    return vars(m)


def kernel(q, tree, *refs):
    (tokens, counts, joint_w, out_w, exp_w, shr_w, cotangent) = refs[:7]
    vectors = refs[7:16]
    (o_out, o_tg, o_vec, o_j, o_o, o_e, o_s) = refs[16:23]
    b = SimpleNamespace(**jax.tree.unflatten(tree, refs[23:]))
    R, D, T, X, RT, n, Y, Z = q.R, q.D, q.T, q.X, q.RT, q.n, q.Y, q.Z
    Dn, DT, F, FB, H, hd, ZT = q.Dn, q.DT, q.F, q.FB, q.H, q.hd, q.ZT
    Cj = 3 * DT

    dp = lax.axis_index("dp")
    s = lax.axis_index("fsdp")
    t = dp % T
    c, xx = t % 2, t // 2
    y, z = s % Y, s // Y
    core = (dp + 1 - 2 * c, s)
    xdp = dp + 2 - 4 * xx
    xpeer = (xdp, s)
    xcore = (xdp + 1 - 2 * c, s)
    tc = t + 1 - 2 * c
    if X == 2:
        tx = t + 2 - 4 * xx
        txc = tx + 1 - 2 * c
    zid = [(z + k) % Z for k in range(Z)]
    zsrc = [(z + Z - k) % Z for k in range(Z)]
    yid = [(y + k) % Y for k in range(Y)]
    ysrc = [(y + Y - k) % Y for k in range(Y)]
    zpeer = [(dp, zid[k] * Y + y) for k in range(Z)]
    ypeer = [(dp, z * Y + yid[k]) for k in range(Y)]
    pending = []

    def rc(src, dst, ss, rs, dev):
        return pltpu.make_async_remote_copy(
            src_ref=src, dst_ref=dst, send_sem=ss, recv_sem=rs,
            device_id=dev, device_id_type=MESH)

    def go(cp):
        cp.start()
        pending.append(cp)
        return cp

    loc = b.loc
    cp_tok = pltpu.make_async_copy(tokens, b.tok.at[t], loc.at[0])
    cp_cot = pltpu.make_async_copy(cotangent, b.cot.at[t], loc.at[1])
    cp_shr = pltpu.make_async_copy(
        shr_w.at[ds(t * FB, FB, 16)], b.w[S].at[ds(s * FB, FB, 16)], loc.at[3])
    cp_j = [pltpu.make_async_copy(
        joint_w.at[:, ds(j * D + t * DT, DT, 128)],
        b.w[J].at[ds(s * Dn, Dn, 16), pl.ds(j * DT, DT)], loc.at[4 + j]) for j in range(3)]
    cp_e = [pltpu.make_async_copy(
        exp_w.at[:, ds(i * (T * FB) + t * FB, FB, 128)],
        b.w[E].at[ds(s * Dn, Dn, 16), pl.ds(i * FB, FB)], loc.at[7 + i]) for i in range(n)]
    for cp in cp_j + [cp_tok] + cp_e + [cp_shr, cp_cot]:
        cp.start()

    lane = lax.broadcasted_iota(jnp.int32, (8, 128), 1)
    cv = jnp.zeros((8, 128), jnp.int32)
    for i in range(q.slots):
        cv = jnp.where(lane == i, counts[0, i], cv)
    b.cnt[t] = cv

    bar = pltpu.get_barrier_semaphore()
    greet = [core] + ([xpeer, xcore] if X == 2 else []) + zpeer[1:] + ypeer[1:]
    for dev in greet:
        pl.semaphore_signal(bar, inc=1, device_id=dev, device_id_type=MESH)
    pl.semaphore_wait(bar, len(greet))

    def slot(w, src_s):
        if w == VEC:
            return b.vec.at[src_s]
        if w == S:
            return b.w[S].at[ds(src_s * FB, FB, 16)]
        return b.w[w].at[ds(src_s * Dn, Dn, 16)]

    def ag_z(w):
        for k in range(1, Z):
            go(rc(slot(w, s), slot(w, s), b.gz[w][0].at[k - 1], b.gz[w][1].at[k - 1], zpeer[k]))

    def ag_y(w, k):
        src = zsrc[k] * Y + y
        if k:
            rc(slot(w, src), slot(w, src), b.gz[w][0].at[k - 1], b.gz[w][1].at[k - 1], zpeer[k]).wait_recv()
        for m in range(1, Y):
            go(rc(slot(w, src), slot(w, src), b.gy[w][0].at[m - 1, k], b.gy[w][1].at[m - 1, k], ypeer[m]))

    def ag_wait(w):
        for k in range(Z):
            for m in range(1, Y):
                src = zsrc[k] * Y + ysrc[m]
                rc(slot(w, src), slot(w, src), b.gy[w][0].at[m - 1, k], b.gy[w][1].at[m - 1, k], ypeer[m]).wait_recv()

    zlo = t * ZT
    mine = z // ZT == t

    def wo_slot(zz, yy):
        return b.w[O].at[ds((zz * Y + yy) * Dn, Dn, 16)]

    def wo_z():
        @pl.when(mine)
        def _():
            zz = z - zlo
            for k in range(1, Z):
                rc(out_w, wo_slot(zz, y), b.gz[O][0].at[k - 1], b.gz[O][1].at[zz], zpeer[k]).start()
            pltpu.make_async_copy(out_w, wo_slot(zz, y), b.gz[O][1].at[zz]).start()

    def wo_y():
        for zz in range(ZT):
            pltpu.make_async_copy(out_w, wo_slot(zz, y), b.gz[O][1].at[zz]).wait()
            for m in range(1, Y):
                go(rc(wo_slot(zz, y), wo_slot(zz, y), b.gy[O][0].at[m - 1, zz], b.gy[O][1].at[m - 1, zz], ypeer[m]))

    def wo_wait():
        for zz in range(ZT):
            for m in range(1, Y):
                rc(wo_slot(zz, ysrc[m]), wo_slot(zz, ysrc[m]), b.gy[O][0].at[m - 1, zz], b.gy[O][1].at[m - 1, zz], ypeer[m]).wait_recv()

    def wo_drain():
        @pl.when(mine)
        def _():
            for k in range(1, Z):
                rc(out_w, wo_slot(z - zlo, y), b.gz[O][0].at[k - 1], b.gz[O][1].at[0], zpeer[k]).wait_send()

    def tp_send(buf, w, src=None):
        src = buf.at[t] if src is None else src
        if X == 2:
            go(rc(src, buf.at[t], w[0].at[1], w[1].at[1], xpeer))
        go(rc(src, buf.at[t], w[0].at[0], w[1].at[0], core))

    def tp_core(buf, w):
        rc(buf.at[tc], buf.at[tc], w[0].at[0], w[1].at[0], core).wait_recv()

    def tp_x(buf, w):
        if X == 2:
            rc(buf.at[tx], buf.at[tx], w[0].at[1], w[1].at[1], xpeer).wait_recv()
            go(rc(buf.at[tx], buf.at[tx], w[0].at[2], w[1].at[2], core))

    def tp_last(buf, w):
        if X == 2:
            rc(buf.at[txc], buf.at[txc], w[0].at[2], w[1].at[2], core).wait_recv()

    order = [(t, None), (tc, tp_core)] + ([(tx, tp_x), (txc, tp_last)] if X == 2 else [])

    vrow = lax.broadcasted_iota(jnp.int32, (VROWS, Dn), 0)
    packed = jnp.zeros((VROWS, Dn), F32)
    pieces = [v[...] for v in vectors[:8]]
    pieces += [vectors[8][pl.ds(r * Dn, Dn)] for r in range(vectors[8].shape[0] // Dn)]
    for i, piece in enumerate(pieces):
        packed = jnp.where(vrow == i, piece.astype(F32).reshape(1, Dn), packed)
    b.vec[s] = packed.astype(BF)
    ag_z(VEC)
    ag_y(VEC, 0)
    cnt = b.cnt
    peers = [core] + ([xpeer, xcore] if X == 2 else [])
    for i, dev in enumerate(peers):
        go(rc(cnt.at[t], cnt.at[t], b.tcnt[0].at[i], b.tcnt[1].at[i], dev))
    for cp in cp_j:
        cp.wait()
    ag_z(J)
    ag_y(J, 0)
    cp_tok.wait()
    tp_send(b.tok, b.ttok)
    wo_z()
    for cp in cp_e:
        cp.wait()
    ag_z(E)
    cp_shr.wait()
    ag_z(S)

    for k in range(1, Z):
        ag_y(VEC, k)
    ag_wait(VEC)
    vf, hb = b.vf, b.hb
    for i in range(n):
        piece = b.vec[i].astype(F32)
        vf[:, i * Dn:(i + 1) * Dn] = piece[0:8]
        kk = FB // Dn
        for r in range(kk):
            row = piece[8 + r:9 + r]
            for g in range(1, T):
                row = jnp.where(t == g, piece[8 + g * kk + r:9 + g * kk + r], row)
            hb[0:1, i * FB + r * Dn:i * FB + (r + 1) * Dn] = row
    vg, vgh = b.vg, b.vgh
    vg[...] = jnp.zeros_like(vg)

    for i, st in enumerate([tc] + ([tx, txc] if X == 2 else [])):
        rc(cnt.at[st], cnt.at[st], b.tcnt[0].at[i], b.tcnt[1].at[i], peers[i]).wait_recv()

    def ends_of(g):
        row = cnt[g]
        ends, total = [], None
        for i in range(q.slots):
            v = row[0:1, i:i + 1]
            total = v if total is None else total + v
            ends.append(total)
        return ends

    RB = 64
    nrb = R // RB

    def live_of(ends, r0, rows):
        places = lax.broadcasted_iota(jnp.int32, (rows, 1), 0) + r0
        return (places < ends[-1]).astype(F32)

    own_ends = ends_of(t)
    cp_cot.wait()
    cot = b.cot

    def cot_step(i, acc):
        r0 = pl.multiple_of(i * RB, RB)
        v = cot[t, pl.ds(r0, RB), :].astype(F32) * live_of(own_ends, r0, RB)
        cot[t, pl.ds(r0, RB), :] = v.astype(BF)
        return acc + jnp.sum(v, axis=0, keepdims=True)

    vg[7:8, :] = lax.fori_loop(0, nrb, cot_step, jnp.zeros((1, D), F32))
    tp_send(cot, b.tcot)

    tok, n1 = b.tok, b.n1

    def ln1(g):
        def step(i, _):
            r0 = pl.multiple_of(i * RB, RB)
            nn, _s = norm_parts(tok[g, pl.ds(r0, RB), :].astype(F32))
            n1[ds(g * R + r0, RB, RB), :] = (nn * vf[0:1, :] + vf[1:2, :]).astype(BF)
            return 0
        lax.fori_loop(0, nrb, step, 0)

    for g, arrive in order:
        if arrive is not None:
            arrive(tok, b.ttok)
        ln1(g)

    for k in range(1, Z):
        ag_y(J, k)
    wo_y()
    ag_y(E, 0)
    tp_core(cot, b.tcot)
    tp_x(cot, b.tcot)
    ag_wait(J)

    qkv, wj = b.qkv, b.w[J]
    TN = 256
    for j in range(3):
        def step(i, _, j=j):
            col = j * DT + i * TN
            r = dot_nn(n1[...], wj[:, ds(col, TN, 128)])
            if j != 1:
                r = r + vf[(2 if j == 0 else 3):(3 if j == 0 else 4), ds(t * DT + i * TN, TN, 128)]
            qkv[:, ds(col, TN, 128)] = r.astype(BF)
            return 0
        lax.fori_loop(0, DT // TN, step, 0)

    scale = hd ** (-0.5)
    prob, mixed = b.prob, b.mixed
    AW = 256
    GH = AW // hd
    lanes = lax.broadcasted_iota(jnp.int32, (1, AW), 1)
    head_masks = [(lanes // hd == h) for h in range(GH)]

    def hm(v, h):
        return jnp.where(head_masks[h], v, jnp.zeros_like(v))

    def attend(g):
        ends = ends_of(g)
        ri = lax.broadcasted_iota(jnp.int32, (R, R), 0)
        ci = lax.broadcasted_iota(jnp.int32, (R, R), 1)
        im_r = jnp.zeros((R, R), jnp.int32)
        im_c = jnp.zeros((R, R), jnp.int32)
        for e in ends:
            im_r = im_r + (ri >= e).astype(jnp.int32)
            im_c = im_c + (ci >= e).astype(jnp.int32)
        same = im_r == im_c
        rows = ds(g * R, R, 256)
        for a in range(DT // AW):
            qa = qkv[rows, pl.ds(a * AW, AW)]
            ka = qkv[rows, pl.ds(DT + a * AW, AW)]
            va = qkv[rows, pl.ds(2 * DT + a * AW, AW)]
            acc = None
            for h in range(GH):
                sc = dot_nt(hm(qa, h), ka) * scale
                sc = jnp.where(same, sc, MASKED)
                top = jnp.max(sc, axis=-1, keepdims=True)
                ex = jnp.exp(sc - top)
                tot = jnp.sum(ex, axis=-1, keepdims=True)
                p = (ex * (1.0 / tot)).astype(BF)
                prob[g * H + a * GH + h] = p
                part = dot_nn(p, hm(va, h))
                acc = part if acc is None else acc + part
            mixed[rows, pl.ds(a * AW, AW)] = acc.astype(BF)

    def att_step(g, _):
        attend(g)
        return 0

    lax.fori_loop(0, T // 2, att_step, 0)
    ag_y(E, 1)
    lax.fori_loop(T // 2, T, att_step, 0)
    wo_wait()

    acc0 = b.acc0

    def block_mm(lhs, g, rhs, nt, put):
        def step(i, _):
            cols = ds(i * TN, TN, 256)
            a = lhs[ds(g * R, R, 256), :]
            put(cols, dot_nt(a, rhs[cols, :]) if nt else dot_nn(a, rhs[:, cols]))
            return 0
        lax.fori_loop(0, D // TN, step, 0)

    def rs_copy(u, r, i):
        return rc(b.psend[u].at[i], b.precv[u].at[i], b.rs[r][0].at[i], b.rs[r][1].at[i], core)

    def rs_xcopy(u, r):
        return rc(b.xsend[u], b.xrecv[u], b.rs[r][2].at[0], b.rs[r][3].at[0], xpeer)

    def rs_start(u, r, lhs, rhs, nt):
        ps = b.psend[u]

        def put_at(i):
            def put(cols, v):
                ps[i, :, cols] = v.astype(BF)
            return put

        def put_acc(cols, v):
            acc0[:, cols] = v

        if X == 2:
            block_mm(lhs, txc, rhs, nt, put_at(1))
            rs_copy(u, r, 1).start()
            block_mm(lhs, tx, rhs, nt, put_acc)
            rs_copy(u, r, 1).wait_recv()
            pr, xs = b.precv[u], b.xsend[u]

            def add(i, _):
                rows = ds(i * RB, RB, RB)
                xs[rows, :] = (acc0[rows, :] + pr[1, rows, :].astype(F32)).astype(BF)
                return 0
            lax.fori_loop(0, nrb, add, 0)
            rs_xcopy(u, r).start()
        block_mm(lhs, tc, rhs, nt, put_at(0))
        rs_copy(u, r, 0).start()
        block_mm(lhs, t, rhs, nt, put_acc)

    def rs_wait(u, r):
        rs_copy(u, r, 0).wait_recv()
        if X == 2:
            rs_xcopy(u, r).wait_recv()

    def rs_value(u, rows):
        v = acc0[rows, :] + b.precv[u][0, rows, :].astype(F32)
        if X == 2:
            v = v + b.xrecv[u][rows, :].astype(F32)
        return v

    def rs_done(u, r):
        for i in range(X):
            rs_copy(u, r, i).wait_send()
        if X == 2:
            rs_xcopy(u, r).wait_send()

    rs_start(0, 0, mixed, b.w[O], False)
    tp_last(cot, b.tcot)
    for k in range(2, Z):
        ag_y(E, k)
    ag_y(S, 0)
    rs_wait(0, 0)
    first, n2 = b.first, b.n2

    def ln2(i, _):
        rows = ds(i * RB, RB, RB)
        v = tok[t, rows, :].astype(F32) + (rs_value(0, rows) + vf[4:5, :])
        first[rows, :] = v
        nn, _s = norm_parts(v)
        n2[t, rows, :] = (nn * vf[5:6, :] + vf[6:7, :]).astype(BF)
        return 0
    lax.fori_loop(0, nrb, ln2, 0)
    tp_send(n2, b.tn2)
    rs_done(0, 0)
    for k in range(1, Z):
        ag_y(S, k)
    ag_wait(E)

    hact, dgelu, we, ws = b.hact, b.dgelu, b.w[E], b.w[S]

    def up(g):
        def step(i, _):
            cols = ds(i * TN, TN, 256)
            rows = ds(g * R, R, 256)
            h = dot_nn(n2[g], we[:, cols]) + hb[0:1, cols]
            phi = 0.5 * (1.0 + lax.erf(h * 0.7071067811865476))
            hact[rows, cols] = (h * phi).astype(BF)
            dgelu[rows, cols] = (phi + h * (jnp.exp(-0.5 * h * h) * 0.3989422804014327)).astype(BF)
            return 0
        lax.fori_loop(0, F // TN, step, 0)

    for g, arrive in order:
        if arrive is not None:
            arrive(n2, b.tn2)
        up(g)

    def blocks(w):
        return q.grads[w]

    def dw_dest(w, k):
        return zlo + k if w == O else zid[k]

    def dw_slot(w, k):
        return k if w == O else zid[k]

    def dw_y(w, sl, m):
        rb = blocks(w)[1]
        return rc(b.dw[w].at[sl, ds(yid[m] * rb, rb, 16)], b.yr[w].at[m - 1, sl],
                  b.sy[w][0].at[m - 1, sl], b.sy[w][1].at[m - 1, sl], ypeer[m])

    def dw_compute(w, k, lhs, rhs):
        bz, rb, C = blocks(w)
        sl = dw_slot(w, k)
        tile = Y * rb
        TC = 256

        def step(i, _):
            cols = ds(i * TC, TC, 256)
            for r in range(tile // 256):
                a = lhs(sl * tile + r * 256)
                b.dw[w][sl, pl.ds(r * 256, 256), cols] = dot_tn(a, rhs(cols)).astype(BF)
            return 0
        lax.fori_loop(0, C // TC, step, 0)
        for m in range(1, Y):
            go(dw_y(w, sl, m))

    def dw_sum(w, k):
        bz, rb, C = blocks(w)
        sl = dw_slot(w, k)
        for m in range(1, Y):
            dw_y(w, sl, m).wait_recv()
        ch = 64

        def add(i, _):
            rows = ds(y * rb + i * ch, ch, 64)
            v = b.dw[w][sl, rows, :].astype(F32)
            for m in range(1, Y):
                v = v + b.yr[w][m - 1, sl, ds(i * ch, ch, 64), :].astype(F32)
            b.dw[w][sl, rows, :] = v.astype(BF)
            return 0
        lax.fori_loop(0, rb // ch, add, 0)

    def dw_z(w, k):
        rb = blocks(w)[1]
        return rc(b.dw[w].at[zid[k], ds(y * rb, rb, 16)], b.zr[w].at[k - 1],
                  b.sz[w][0].at[k - 1], b.sz[w][1].at[k - 1], zpeer[k])

    def dw_o(zz, k):
        return rc(b.dw[O].at[zz, ds(y * Dn, Dn, 16)], b.zr[O].at[k - 1],
                  b.sz[O][0].at[k - 1], b.sz[O][1].at[k - 1], zpeer[k])

    def dw_send(w, k):
        dw_sum(w, k)
        if k:
            go(dw_z(w, k))

    def dwo_send(drain=False):
        for zz in range(ZT):
            if not drain:
                dw_sum(O, zz)
            for k in range(1, Z):
                @pl.when(zid[k] == zlo + zz)
                def _(zz=zz, k=k):
                    if drain:
                        dw_o(zz, k).wait_send()
                    else:
                        dw_o(zz, k).start()

    def dw_final(w):
        bz, rb, C = blocks(w)
        for k in range(1, Z):
            (dw_o(0, k) if w == O else dw_z(w, k)).wait_recv()
        ch = 64
        fin = b.fin[w]
        own = z - zlo if w == O else z
        me = 0 if w == O else t

        def add(i, _):
            rows = ds(i * ch, ch, 64)
            v = b.dw[w][own, ds(y * rb + i * ch, ch, 64), :].astype(F32)
            for k in range(1, Z):
                v = v + b.zr[w][k - 1, rows, :].astype(F32)
            fin[me, rows, :] = v.astype(BF)
            return 0
        lax.fori_loop(0, rb // ch, add, 0)
        if w != O:
            tp_send(fin, b.tfin[w])

    def out_copies(w, g):
        fin, so = b.fin[w], b.sout[w]
        if w == J:
            return [pltpu.make_async_copy(fin.at[g, :, pl.ds(j * DT, DT)],
                    o_j.at[:, ds(j * D + g * DT, DT, 128)], so.at[g, j]) for j in range(3)]
        if w == E:
            return [pltpu.make_async_copy(fin.at[g, :, pl.ds(i * FB, FB)],
                    o_e.at[:, ds(i * (T * FB) + g * FB, FB, 128)], so.at[g, i]) for i in range(n)]
        return [pltpu.make_async_copy(fin.at[g], o_s.at[ds(g * FB, FB, 16)], so.at[g, 0])]

    def cot_rhs(cols):
        return cot[:, :, cols].reshape(RT, 256)

    for k in list(range(1, Z)) + [0]:
        dw_compute(S, k, lambda c0: hact[:, ds(c0, 256, 256)], cot_rhs)

    ag_wait(S)
    hgrad = b.hgrad

    def down(g, acc):
        def step(i, _):
            cols = ds(i * TN, TN, 256)
            rows = ds(g * R, R, 256)
            v = dot_nt(cot[g], ws[cols, :]) * dgelu[rows, cols].astype(F32)
            hgrad[rows, cols] = v.astype(BF)
            return 0
        lax.fori_loop(0, F // TN, step, 0)
        return acc

    lax.fori_loop(0, T, down, 0)
    rs_start(0, 1, hgrad, we, True)
    dw_send(S, 1)

    for k in list(range(1, Z)) + [0]:
        dw_compute(E, k, lambda c0: n2[:, :, ds(c0, 256, 256)].reshape(RT, 256), lambda cols: hgrad[:, cols])
    dw_send(S, 2) if Z > 2 else None

    rs_wait(0, 1)
    proj, fgrad = b.proj, b.fgrad

    def ln2_back(i, carry):
        ag_, as_, ab_ = carry
        rows = ds(i * RB, RB, RB)
        two = rs_value(0, rows)
        nn, sd = norm_parts(first[rows, :])
        e = two * vf[5:6, :]
        og = cot[t, rows, :].astype(F32)
        fg = og + sd * (e - jnp.mean(e, axis=-1, keepdims=True)
                        - nn * jnp.mean(e * nn, axis=-1, keepdims=True))
        fgrad[rows, :] = fg
        pj = fg.astype(BF)
        proj[t, rows, :] = pj
        return (ag_ + jnp.sum(two * nn, axis=0, keepdims=True),
                as_ + jnp.sum(two, axis=0, keepdims=True),
                ab_ + jnp.sum(pj.astype(F32), axis=0, keepdims=True))

    zrow = jnp.zeros((1, D), F32)
    g2, s2, ob = lax.fori_loop(0, nrb, ln2_back, (zrow, zrow, zrow))
    tp_send(proj, b.tproj)
    vg[5:6, :] = g2
    vg[6:7, :] = s2
    vg[4:5, :] = ob
    rs_done(0, 1)

    rs_start(1, 2, hact, ws, False)

    def hb_step(i, _):
        cols = ds(i * TN, TN, 256)
        vgh[0:1, cols] = jnp.sum(hgrad[:, cols].astype(F32), axis=0, keepdims=True)
        return 0
    lax.fori_loop(0, F // TN, hb_step, 0)
    dw_send(S, 3) if Z > 3 else None

    mgrad, jgrad, wo = b.mgrad, b.jgrad, b.w[O]

    def mixed_back(g):
        def step(i, _):
            cols = ds(i * TN, TN, 256)
            mgrad[ds(g * R, R, 256), cols] = dot_nt(proj[g], wo[cols, :]).astype(BF)
            return 0
        lax.fori_loop(0, DT // TN, step, 0)

    def attend_back(g):
        rows = ds(g * R, R, 256)
        for a in range(DT // AW):
            qa = qkv[rows, pl.ds(a * AW, AW)]
            ka = qkv[rows, pl.ds(DT + a * AW, AW)]
            va = qkv[rows, pl.ds(2 * DT + a * AW, AW)]
            ma = mgrad[rows, pl.ds(a * AW, AW)]
            aq = ak = av = None
            for h in range(GH):
                mh = hm(ma, h)
                pg = dot_nt(mh, va)
                pl_ = prob[g * H + a * GH + h]
                p = pl_.astype(F32)
                inner = jnp.sum(p * pg, axis=-1, keepdims=True)
                sg = (p * (pg - inner)).astype(BF)
                dq = dot_nn(sg, hm(ka, h))
                dk = dot_tn(sg, hm(qa, h))
                dv = dot_tn(pl_, mh)
                aq = dq if aq is None else aq + dq
                ak = dk if ak is None else ak + dk
                av = dv if av is None else av + dv
            jgrad[rows, pl.ds(a * AW, AW)] = (aq * scale).astype(BF)
            jgrad[rows, pl.ds(DT + a * AW, AW)] = (ak * scale).astype(BF)
            jgrad[rows, pl.ds(2 * DT + a * AW, AW)] = av.astype(BF)

    rs_wait(1, 2)
    obuf = b.obuf

    def out_step(i, _):
        rows = ds(i * RB, RB, RB)
        r0 = i * RB
        v = (first[rows, :] + rs_value(1, rows) + vf[7:8, :]) * live_of(own_ends, r0, RB)
        obuf[rows, :] = v.astype(BF)
        return 0
    lax.fori_loop(0, nrb, out_step, 0)
    cp_out = pltpu.make_async_copy(obuf, o_out, loc.at[0])
    cp_out.start()

    for g, arrive in order:
        if arrive is not None:
            arrive(proj, b.tproj)
        mixed_back(g)

    for zz in range(ZT):
        dw_compute(O, zz, lambda c0: mixed[:, ds(c0, 256, 256)],
                   lambda cols: proj[:, :, cols].reshape(RT, 256))

    def attb_step(g, _):
        attend_back(g)
        return 0
    lax.fori_loop(0, T // 2, attb_step, 0)
    dw_send(S, 0)
    dw_send(E, 1)
    lax.fori_loop(T // 2, T, attb_step, 0)
    dw_send(E, 2) if Z > 2 else None

    for k in list(range(1, Z)) + [0]:
        dw_compute(J, k, lambda c0: n1[:, ds(c0, 256, 256)], lambda cols: jgrad[:, cols])
    rs_start(0, 3, jgrad, wj, True)
    dw_send(E, 3) if Z > 3 else None
    dw_send(E, 0)
    dw_final(S)
    for i in range(2):
        j = 2 * i
        vg[2 + i:3 + i, ds(t * DT, DT, 128)] = jnp.sum(
            jgrad[:, pl.ds(j * DT, DT)].astype(F32), axis=0, keepdims=True)
    dwo_send()

    rs_wait(0, 3)
    tbuf = b.tbuf

    def ln1_back(i, carry):
        ag_, as_ = carry
        rows = ds(i * RB, RB, RB)
        one = rs_value(0, rows)
        nn, sd = norm_parts(tok[t, rows, :].astype(F32))
        e = one * vf[0:1, :]
        v = fgrad[rows, :] + sd * (e - jnp.mean(e, axis=-1, keepdims=True)
                                   - nn * jnp.mean(e * nn, axis=-1, keepdims=True))
        tbuf[rows, :] = v.astype(BF)
        return (ag_ + jnp.sum(one * nn, axis=0, keepdims=True),
                as_ + jnp.sum(one, axis=0, keepdims=True))

    g1, s1 = lax.fori_loop(0, nrb, ln1_back, (zrow, zrow))
    cp_tg = pltpu.make_async_copy(tbuf, o_tg, loc.at[1])
    cp_tg.start()
    vg[0:1, :] = g1
    vg[1:2, :] = s1

    v3, v3c = b.v3, b.v3c
    kk = FB // Dn
    v3[...] = jnp.zeros_like(v3)
    for i in range(n):
        v3[i, 0:8, :] = vg[:, i * Dn:(i + 1) * Dn]
        for r in range(kk):
            row = vgh[0:1, i * FB + r * Dn:i * FB + (r + 1) * Dn]
            for g in range(T):
                v3[i, 8 + g * kk + r:9 + g * kk + r, :] = jnp.where(t == g, row, jnp.zeros_like(row))
    vt = [rc(v3, v3c.at[0], b.svt[0].at[0], b.svt[1].at[0], core)]
    vt[0].start()
    vt[0].wait()
    v3[...] = v3[...] + v3c[0]
    if X == 2:
        vx = rc(v3, v3c.at[1], b.svt[0].at[1], b.svt[1].at[1], xpeer)
        vx.start()
        vx.wait()
        v3[...] = v3[...] + v3c[1]
    v3y, v3s, v3z = b.v3y, b.v3s, b.v3z

    def vy(m, k):
        return rc(v3.at[zid[k] * Y + yid[m]], v3y.at[m - 1, zid[k]], b.svy[0].at[m - 1, zid[k]],
                  b.svy[1].at[m - 1, zid[k]], ypeer[m])
    for k in range(Z):
        for m in range(1, Y):
            go(vy(m, k))

    dw_send(J, 1)

    def vz(k):
        return rc(v3s.at[k], v3z.at[k - 1], b.svz[0].at[k - 1], b.svz[1].at[k - 1], zpeer[k])
    for k in list(range(1, Z)) + [0]:
        v = v3[zid[k] * Y + y]
        for m in range(1, Y):
            vy(m, k).wait_recv()
            v = v + v3y[m - 1, zid[k]]
        v3s[k] = v
        if k:
            go(vz(k))

    for k in range(2, Z):
        dw_send(J, k)
    dw_send(J, 0)

    copies = []

    def emit(w, g):
        for cp in out_copies(w, g):
            cp.start()
            copies.append(cp)

    dw_final(E)

    @pl.when(mine)
    def _():
        dw_final(O)
        for i, dev in enumerate(peers):
            rc(b.fin[O].at[0], b.fin[O].at[0], b.tfo[0].at[i], b.tfo[1].at[0], dev).start()

    for w in (S, E):
        emit(w, t)
        tp_core(b.fin[w], b.tfin[w])
        emit(w, tc)
        tp_x(b.fin[w], b.tfin[w])
        if X == 2:
            emit(w, tx)

    v = v3s[0]
    for k in range(1, Z):
        vz(k).wait_recv()
        v = v + v3z[k - 1]
    b.vout[...] = v
    cp_v = pltpu.make_async_copy(b.vout, o_vec, loc.at[2])
    cp_v.start()

    dw_final(J)
    for w in (S, E):
        tp_last(b.fin[w], b.tfin[w])
        if X == 2:
            emit(w, txc)

    @pl.when(jnp.logical_not(mine))
    def _():
        rc(b.fin[O].at[0], b.fin[O].at[0], b.tfo[0].at[0], b.tfo[1].at[0], core).wait_recv()
    cp_o = pltpu.make_async_copy(b.fin[O].at[0], o_o, loc.at[3])
    cp_o.start()
    w = J
    emit(w, t)
    tp_core(b.fin[w], b.tfin[w])
    emit(w, tc)
    tp_x(b.fin[w], b.tfin[w])
    tp_last(b.fin[w], b.tfin[w])
    if X == 2:
        emit(w, tx)
        emit(w, txc)

    for cp in pending:
        cp.wait_send()
    for u, r in ((1, 2), (0, 3)):
        rs_done(u, r)
    wo_drain()
    dwo_send(drain=True)

    @pl.when(mine)
    def _():
        for i, dev in enumerate(peers):
            rc(b.fin[O].at[0], b.fin[O].at[0], b.tfo[0].at[i], b.tfo[1].at[0], dev).wait_send()
    for cp in copies + [cp_out, cp_tg, cp_v, cp_o]:
        cp.wait()


def finish(divisor, q, *refs):
    ins, outs = refs[:7], refs[7:]
    for i in range(2):
        outs[i][...] = ins[i][...]
    for i in range(2, 6):
        outs[i][...] = ins[i][...].astype(F32) * (1.0 / divisor)

    @pl.when(pl.program_id(0) == 0)
    def _():
        v = ins[6][...] * (1.0 / divisor)
        for i in range(8):
            outs[6 + i][...] = v[i]
        for r in range(q.FF // q.D):
            outs[14][pl.ds(r * q.Dn, q.Dn)] = v[8 + r]


def body(n_dp, n_fsdp, tokens, patch_counts, gain_one, shift_one, joint_w, query_b, value_b, out_w,
         out_b, gain_two, shift_two, expand_w, expand_b, shrink_w, shrink_b, cotangent):
    R, D = tokens.shape
    q = Sizes(n_dp, n_fsdp, R, D, expand_w.shape[1], patch_counts.shape[1])
    q.grads = [(q.Z, q.Dn, 3 * q.DT), (q.ZT, q.Dn, D), (q.Z, q.Dn, q.F), (q.Z, q.FB, D)]
    scratch, tree = jax.tree.flatten(layout(q))
    anyspec = pl.BlockSpec(memory_space=pl.ANY)
    vmem = pl.BlockSpec(memory_space=pltpu.VMEM)
    sds = jax.ShapeDtypeStruct
    outs = pl.pallas_call(
        functools.partial(kernel, q, tree),
        out_shape=(
            sds((R, D), BF), sds((R, D), BF), sds((VROWS, q.Dn), F32),
            sds((q.Dn, 3 * D), BF), sds((q.Dn, D), BF), sds((q.Dn, q.FF), BF),
            sds((q.FF // q.n, D), BF)),
        in_specs=[anyspec, pl.BlockSpec(memory_space=pltpu.SMEM)] + [anyspec] * 5 + [vmem] * 9,
        out_specs=tuple([anyspec] * 7),
        scratch_shapes=scratch,
        compiler_params=pltpu.CompilerParams(
            collective_id=0, has_side_effects=True, vmem_limit_bytes=67043328),
        name="layer",
    )(tokens, patch_counts, joint_w, out_w, expand_w, shrink_w, cotangent,
      gain_one, shift_one, query_b, value_b, out_b, gain_two, shift_two, shrink_b, expand_b)
    result, tokens_grad, vec, gj, go_, ge, gs = outs
    divisor = float(n_dp * n_fsdp)
    mats = [gj, go_, ge, gs]
    if n_dp > q.T:
        groups = [[i + q.T * g for g in range(n_dp // q.T)] for i in range(q.T)]
        summed = lax.psum(tuple([vec] + mats), "dp", axis_index_groups=groups)
        vec, mats = summed[0], list(summed[1:])
    steps = 4
    blocked = lambda v: pl.BlockSpec((v.shape[0] // steps, v.shape[1]), lambda i: (i, 0))
    rows_in = [result, tokens_grad] + mats
    small = [q.Dn] * 8 + [q.FF // q.n]
    done = pl.pallas_call(
        functools.partial(finish, divisor, q),
        grid=(steps,),
        out_shape=tuple([sds(v.shape, BF) for v in rows_in[:2]] + [sds(v.shape, F32) for v in mats]
                        + [sds((k,), F32) for k in small]),
        in_specs=[blocked(v) for v in rows_in] + [vmem],
        out_specs=tuple([blocked(v) for v in rows_in] + [vmem] * 9),
        name="finish",
    )(*rows_in, vec)
    result, tokens_grad, gj, go_, ge, gs = done[:6]
    vec = done[6:]
    return (result, tokens_grad, vec[0], vec[1], gj, vec[2], vec[3], go_, vec[4], vec[5], vec[6],
            ge, vec[8], gs, vec[7])


def solution(mesh):
    rows = P(("dp", "fsdp"), None)
    vec, mat = P("fsdp"), P("fsdp", None)
    in_specs = (rows, rows, vec, vec, mat, vec, vec, mat, vec, vec, vec, mat, vec, mat, vec, rows)
    out_specs = (rows, rows, vec, vec, mat, vec, vec, mat, vec, vec, vec, mat, vec, mat, vec)
    fn = functools.partial(body, mesh.shape["dp"], mesh.shape["fsdp"])
    return jax.shard_map(fn, mesh=mesh, in_specs=in_specs, out_specs=out_specs, check_vma=False)
```

time: 1010 us -> 234 us (0.23)
  waiting for transfers between devices: 686 us -> 0 us
  Pallas kernels: 0 us -> 231 us
  blocking collectives: 186 us -> 0 us
  matrix products: 82.7 us -> 0 us
  other arithmetic: 20.5 us -> 0 us
  between operations: 16 us -> 0.82 us
  local copies, waits for them, and re-layouts: 10.2 us -> 0 us
    reduce_scatter x4 -> x0, waiting for transfers between devices: 385 us -> none  [the longest x1 151 us: body(): lax.psum_scatter(mlp_terms[2].astype(jnp.bfloat16), 'fsdp', scatter_dimen...]
    all_gather x4 -> x0, waiting for transfers between devices: 239 us -> none  [the longest x1 124 us: body(): lax.all_gather(expand_weight, 'fsdp', axis=0, tiled=True)]
    pallas_call x0 -> x2, Pallas kernels: none -> 231 us  [the longest x1 225 us: body(): pl.pallas_call(functools.partial(kernel, q, tree), out_shape=(sds((R, D),...]
    all_gather x9 -> x0, blocking collectives: 142 us -> none  [the longest x1 22.4 us: body(): lax.all_gather(expand_bias, 'fsdp', axis=0, tiled=True)]
    dot_general x18 -> x0, matrix products: 82.7 us -> none  [the longest x4 30.5 us: full_dot(): return jnp.dot(left, right, preferred_element_type=jnp.float32)]
    psum x1 -> x0, waiting for transfers between devices: 58.8 us -> none  [body(): lax.psum(attn_shards[2].astype(jnp.bfloat16), 'dp').astype(jnp.float32)]
    unnamed x1 -> x0, blocking collectives: 26.6 us -> none
    psum x1 -> x0, blocking collectives: 17.3 us -> none  [body(): lax.psum(attn_shards[0].astype(jnp.bfloat16), 'dp').astype(jnp.float32)]
  transfers between devices with their start and end apart: 9 -> 0, of which waited for: 7 -> 0; matrix products, arithmetic and copies ran while one was open for 8% -> 0% of each run, Pallas kernels for 0% -> 0%
where the time goes in v1:
time: 234 us; the launch traced here: 231 us
  Pallas kernels  231 us (99%)
    pallas_call x1, Pallas kernels, body(): pl.pallas_call(functools.partial(kernel, q, tree), out_shape=(sds((R, D),...  225 us
    pallas_call x1, Pallas kernels, body(): pl.pallas_call(functools.partial(finish, divisor, q), grid=(steps,), out_...  5.72 us

profile of v1, /device:TPU:3, one launch (start us, length us, event | category | flops | bytes accessed | tf_op | source)
XLA Modules:
  0.0 231.3 jit_solution(17267127008100158923)
XLA Ops:
  0.7 224.8 %layer.1 = (bf16[256,1024]{1,0:T(8,128)(2,1)}, bf16[256,1024]{1,0:T(8,128)(2,1)}, f32[16,128]{1,0:T(8,128)}, bf16[128,3072]{1,0:T(8,128)(2,1)}, bf16[128,1024]{1...) custom-call(bf16[256,1024]{1,0:T(8,128)(2,1)} %refs_0_.1, s32[1,4]{1,0:T(1,128)} %refs_1_.1, ...), custom_call_target="tpu_custom_call" | custom-call | tf_op jit(solution)/shard_map/layer/pallas_call | solution.py:923
  225.5 5.7 %finish.1 = (bf16[256,1024]{1,0:T(8,128)(2,1)}, bf16[256,1024]{1,0:T(8,128)(2,1)}, f32[128,3072]{1,0:T(8,128)}, f32[128,1024]{1,0:T(8,128)}, f32[128,4096]{1,0:T...) custom-call(bf16[256,1024]{1,0:T(8,128)(2,1)} %get-tuple-element.37., ...), custom_call_target="tpu_custom_call" | custom-call | tf_op jit(solution)/shard_map/finish/pallas_call | solution.py:948

commit v2 on v1

--- a/solution.py
+++ b/solution.py
@@ -52,6 +52,15 @@
 
 def ds(start, size, mult):
     return pl.ds(pl.multiple_of(start, mult), size)
+
+
+def flip(v, k):
+    r, bit = v, 1
+    while bit <= k:
+        if k & bit:
+            r = r + bit - 2 * bit * (v // bit % 2)
+        bit *= 2
+    return r
 
 
 def norm_parts(x):
@@ -84,8 +93,6 @@
     m.fgrad = V((R, D), F32)
     m.mgrad = V((RT, q.DT), BF)
     m.jgrad = V((RT, Cj), BF)
-    m.obuf = V((R, D), BF)
-    m.tbuf = V((R, D), BF)
     m.acc0 = V((R, D), F32)
     m.psend = [V((q.X, R, D), BF) for _ in range(2)]
     m.precv = [V((q.X, R, D), BF) for _ in range(2)]
@@ -95,11 +102,12 @@
     m.dw = [V((bz, q.Y * rb, C), BF) for bz, rb, C in q.grads]
     m.yr = [V((q.Y - 1, bz, rb, C), BF) for bz, rb, C in q.grads]
     m.zr = [V((q.Z - 1, rb, C), BF) for bz, rb, C in q.grads]
+    m.zq = [V((16, 128) if w == O else (rb, C), BF) for w, (bz, rb, C) in enumerate(q.grads)]
     m.fin = [V((1 if w == O else T, rb, C), BF) for w, (bz, rb, C) in enumerate(q.grads)]
     m.sy = [[DMA((q.Y - 1, bz)), DMA((q.Y - 1, bz))] for bz, rb, C in q.grads]
-    m.sz = [[DMA((q.Z - 1,)), DMA((q.Z - 1,))] for _ in q.grads]
+    m.sz = [[DMA((q.Z - 1,)), DMA((q.Z,))] for _ in q.grads]
     m.sout = [DMA((T, q.n)) for _ in q.grads]
-    m.gz = [[DMA((q.Z - 1,)), DMA((max(q.Z - 1, q.ZT),))] for _ in range(5)]
+    m.gz = [[DMA((q.Z,)), DMA((max(q.Z - 1, q.ZT),))] for _ in range(5)]
     m.gy = [[DMA((q.Y - 1, q.Z)), DMA((q.Y - 1, q.Z))] for _ in range(5)]
     pair = lambda: [DMA((3,)), DMA((3,))]
     m.ttok, m.tcot, m.tn2, m.tproj, m.tcnt, m.tfo = (pair() for _ in range(6))
@@ -145,13 +153,16 @@
     if X == 2:
         tx = t + 2 - 4 * xx
         txc = tx + 1 - 2 * c
-    zid = [(z + k) % Z for k in range(Z)]
-    zsrc = [(z + Z - k) % Z for k in range(Z)]
+    zid = [flip(z, k) for k in range(Z)]
+    relay = Z == 4
+    inner = jnp.logical_and(z > 0, z < Z - 1)
+    outer = jnp.logical_not(inner)
+    zfar = jnp.where(z > 1, Z - 1, 0)
     yid = [(y + k) % Y for k in range(Y)]
     ysrc = [(y + Y - k) % Y for k in range(Y)]
     zpeer = [(dp, zid[k] * Y + y) for k in range(Z)]
     ypeer = [(dp, z * Y + yid[k]) for k in range(Y)]
-    pending = []
+    pending, pending_if = [], []
 
     def rc(src, dst, ss, rs, dev):
         return pltpu.make_async_remote_copy(
@@ -162,6 +173,10 @@
         cp.start()
         pending.append(cp)
         return cp
+
+    def go_if(pred, cp):
+        pl.when(pred)(cp.start)
+        pending_if.append((pred, cp))
 
     loc = b.loc
     cp_tok = pltpu.make_async_copy(tokens, b.tok.at[t], loc.at[0])
@@ -196,21 +211,60 @@
             return b.w[S].at[ds(src_s * FB, FB, 16)]
         return b.w[w].at[ds(src_s * Dn, Dn, 16)]
 
+    def gz_copy(w, k):
+        return rc(slot(w, s), slot(w, s), b.gz[w][0].at[k - 1], b.gz[w][1].at[k - 1], zpeer[k])
+
+    def gz_wait(w, k):
+        src = slot(w, zid[k] * Y + y)
+        rc(src, src, b.gz[w][0].at[k - 1], b.gz[w][1].at[k - 1], zpeer[k]).wait_recv()
+
+    def gy_copies(w, k):
+        src = slot(w, zid[k] * Y + y)
+        return [rc(src, src, b.gy[w][0].at[m - 1, k], b.gy[w][1].at[m - 1, k], ypeer[m])
+                for m in range(1, Y)]
+
     def ag_z(w):
-        for k in range(1, Z):
-            go(rc(slot(w, s), slot(w, s), b.gz[w][0].at[k - 1], b.gz[w][1].at[k - 1], zpeer[k]))
+        if not relay or w == VEC:
+            for k in range(1, Z):
+                go(gz_copy(w, k))
+            return
+        go(gz_copy(w, 1))
+        go_if(inner, gz_copy(w, 3))
+        go(gz_copy(w, 2))
 
     def ag_y(w, k):
-        src = zsrc[k] * Y + y
         if k:
-            rc(slot(w, src), slot(w, src), b.gz[w][0].at[k - 1], b.gz[w][1].at[k - 1], zpeer[k]).wait_recv()
-        for m in range(1, Y):
-            go(rc(slot(w, src), slot(w, src), b.gy[w][0].at[m - 1, k], b.gy[w][1].at[m - 1, k], ypeer[m]))
+            gz_wait(w, k)
+        if relay and w != VEC and k == 2:
+            src = slot(w, zid[k] * Y + y)
+            go_if(inner, rc(src, src, b.gz[w][0].at[Z - 1], b.gz[w][1].at[2], (dp, zfar * Y + y)))
+        for cp in gy_copies(w, k):
+            go(cp)
+
+    def ag_y_if(pred, w, k):
+        @pl.when(pred)
+        def _():
+            gz_wait(w, k)
+            for cp in gy_copies(w, k):
+                cp.start()
+
+    def fw(w, *steps):
+        for i in steps:
+            if not relay or w == VEC:
+                if i < Z:
+                    ag_y(w, i)
+            elif i == 2:
+                ag_y_if(inner, w, 3)
+            elif i == 4:
+                ag_y_if(outer, w, 3)
+                pending.extend(gy_copies(w, 3))
+            else:
+                ag_y(w, {0: 0, 1: 1, 3: 2}[i])
 
     def ag_wait(w):
         for k in range(Z):
             for m in range(1, Y):
-                src = zsrc[k] * Y + ysrc[m]
+                src = zid[k] * Y + ysrc[m]
                 rc(slot(w, src), slot(w, src), b.gy[w][0].at[m - 1, k], b.gy[w][1].at[m - 1, k], ypeer[m]).wait_recv()
 
     zlo = t * ZT
@@ -280,18 +334,13 @@
     for cp in cp_j:
         cp.wait()
     ag_z(J)
-    ag_y(J, 0)
+    fw(J, 0)
     cp_tok.wait()
     tp_send(b.tok, b.ttok)
     wo_z()
-    for cp in cp_e:
-        cp.wait()
-    ag_z(E)
-    cp_shr.wait()
-    ag_z(S)
-
-    for k in range(1, Z):
-        ag_y(VEC, k)
+    last = range(4, max(Z, 5))
+
+    fw(VEC, *range(1, Z))
     ag_wait(VEC)
     vf, hb = b.vf, b.hb
     for i in range(n):
@@ -348,17 +397,22 @@
             return 0
         lax.fori_loop(0, nrb, step, 0)
 
-    for g, arrive in order:
-        if arrive is not None:
-            arrive(tok, b.ttok)
-        ln1(g)
-
-    for k in range(1, Z):
-        ag_y(J, k)
-    wo_y()
-    ag_y(E, 0)
-    tp_core(cot, b.tcot)
-    tp_x(cot, b.tcot)
+    ln1(t)
+    tp_core(tok, b.ttok)
+    ln1(tc)
+    fw(J, 1)
+    tp_x(tok, b.ttok)
+    fw(J, 2)
+    if X == 2:
+        ln1(tx)
+        tp_last(tok, b.ttok)
+        ln1(txc)
+    fw(J, 3)
+    fw(J, *last)
+    for cp in cp_e:
+        cp.wait()
+    ag_z(E)
+    fw(E, 0)
     ag_wait(J)
 
     qkv, wj = b.qkv, b.w[J]
@@ -415,9 +469,11 @@
         attend(g)
         return 0
 
-    lax.fori_loop(0, T // 2, att_step, 0)
-    ag_y(E, 1)
-    lax.fori_loop(T // 2, T, att_step, 0)
+    lax.fori_loop(0, T, att_step, 0)
+    wo_y()
+    cp_shr.wait()
+    ag_z(S)
+    fw(E, 1)
     wo_wait()
 
     acc0 = b.acc0
@@ -482,10 +538,10 @@
             rs_xcopy(u, r).wait_send()
 
     rs_start(0, 0, mixed, b.w[O], False)
-    tp_last(cot, b.tcot)
-    for k in range(2, Z):
-        ag_y(E, k)
-    ag_y(S, 0)
+    tp_core(cot, b.tcot)
+    tp_x(cot, b.tcot)
+    fw(E, 2)
+    fw(E, 3)
     rs_wait(0, 0)
     first, n2 = b.first, b.n2
 
@@ -498,9 +554,10 @@
         return 0
     lax.fori_loop(0, nrb, ln2, 0)
     tp_send(n2, b.tn2)
+    fw(E, *last)
+    fw(S, 0)
     rs_done(0, 0)
-    for k in range(1, Z):
-        ag_y(S, k)
+    tp_last(cot, b.tcot)
     ag_wait(E)
 
     hact, dgelu, we, ws = b.hact, b.dgelu, b.w[E], b.w[S]
@@ -516,10 +573,18 @@
             return 0
         lax.fori_loop(0, F // TN, step, 0)
 
-    for g, arrive in order:
-        if arrive is not None:
-            arrive(n2, b.tn2)
-        up(g)
+    up(t)
+    tp_core(n2, b.tn2)
+    up(tc)
+    fw(S, 1)
+    tp_x(n2, b.tn2)
+    if X == 2:
+        up(tx)
+        tp_last(n2, b.tn2)
+        up(txc)
+    fw(S, 2)
+    fw(S, 3)
+    fw(S, *last)
 
     def blocks(w):
         return q.grads[w]
@@ -576,8 +641,29 @@
         return rc(b.dw[O].at[zz, ds(y * Dn, Dn, 16)], b.zr[O].at[k - 1],
                   b.sz[O][0].at[k - 1], b.sz[O][1].at[k - 1], zpeer[k])
 
+    def dw_relay(w):
+        rb = blocks(w)[1]
+        return rc(b.dw[w].at[zid[3], ds(y * rb, rb, 16)], b.zq[w], b.sz[w][0].at[2],
+                  b.sz[w][1].at[Z - 1], zpeer[1])
+
     def dw_send(w, k):
         dw_sum(w, k)
+        if relay and k == 3:
+            go_if(inner, dw_z(w, k))
+            go_if(outer, dw_relay(w))
+            return
+        if relay and k == 2:
+            @pl.when(inner)
+            def _():
+                dw_relay(w).wait_recv()
+                rb, ch = blocks(w)[1], 64
+
+                def add(i, _):
+                    rows = ds(y * rb + i * ch, ch, 64)
+                    v = b.dw[w][zid[2], rows, :].astype(F32) + b.zq[w][ds(i * ch, ch, 64), :].astype(F32)
+                    b.dw[w][zid[2], rows, :] = v.astype(BF)
+                    return 0
+                lax.fori_loop(0, rb // ch, add, 0)
         if k:
             go(dw_z(w, k))
 
@@ -595,21 +681,29 @@
 
     def dw_final(w):
         bz, rb, C = blocks(w)
-        for k in range(1, Z):
-            (dw_o(0, k) if w == O else dw_z(w, k)).wait_recv()
         ch = 64
         fin = b.fin[w]
         own = z - zlo if w == O else z
         me = 0 if w == O else t
 
-        def add(i, _):
-            rows = ds(i * ch, ch, 64)
-            v = b.dw[w][own, ds(y * rb + i * ch, ch, 64), :].astype(F32)
-            for k in range(1, Z):
-                v = v + b.zr[w][k - 1, rows, :].astype(F32)
-            fin[me, rows, :] = v.astype(BF)
-            return 0
-        lax.fori_loop(0, rb // ch, add, 0)
+        def total(ks):
+            for k in ks:
+                (dw_o(0, k) if w == O else dw_z(w, k)).wait_recv()
+
+            def add(i, _):
+                rows = ds(i * ch, ch, 64)
+                v = b.dw[w][own, ds(y * rb + i * ch, ch, 64), :].astype(F32)
+                for k in ks:
+                    v = v + b.zr[w][k - 1, rows, :].astype(F32)
+                fin[me, rows, :] = v.astype(BF)
+                return 0
+            lax.fori_loop(0, rb // ch, add, 0)
+
+        if relay and w != O:
+            pl.when(inner)(lambda: total((1, 2, 3)))
+            pl.when(outer)(lambda: total((1, 2)))
+        else:
+            total(range(1, Z))
         if w != O:
             tp_send(fin, b.tfin[w])
 
@@ -626,9 +720,15 @@
     def cot_rhs(cols):
         return cot[:, :, cols].reshape(RT, 256)
 
-    for k in list(range(1, Z)) + [0]:
-        dw_compute(S, k, lambda c0: hact[:, ds(c0, 256, 256)], cot_rhs)
-
+    zorder = ([3, 1, 2] if relay else list(range(1, Z))) + [0]
+    half = len(zorder) // 2
+
+    def dw_shrink(ks):
+        for k in ks:
+            dw_compute(S, k, lambda c0: hact[:, ds(c0, 256, 256)], cot_rhs)
+
+    dw_shrink(zorder[:half])
+    dw_shrink(zorder[half:])
     ag_wait(S)
     hgrad = b.hgrad
 
@@ -643,13 +743,23 @@
         return acc
 
     lax.fori_loop(0, T, down, 0)
+    def send(w, *steps):
+        for i in steps:
+            if i < Z:
+                dw_send(w, zorder[i])
+
+    send(S, 0)
     rs_start(0, 1, hgrad, we, True)
-    dw_send(S, 1)
-
-    for k in list(range(1, Z)) + [0]:
-        dw_compute(E, k, lambda c0: n2[:, :, ds(c0, 256, 256)].reshape(RT, 256), lambda cols: hgrad[:, cols])
-    dw_send(S, 2) if Z > 2 else None
-
+    send(S, 1)
+
+    def dw_expand(ks):
+        for k in ks:
+            dw_compute(E, k, lambda c0: n2[:, :, ds(c0, 256, 256)].reshape(RT, 256),
+                       lambda cols: hgrad[:, cols])
+
+    dw_expand(zorder[:half])
+    send(S, 2)
+    dw_expand(zorder[half:])
     rs_wait(0, 1)
     proj, fgrad = b.proj, b.fgrad
 
@@ -677,6 +787,7 @@
     vg[4:5, :] = ob
     rs_done(0, 1)
 
+    send(S, *range(3, Z))
     rs_start(1, 2, hact, ws, False)
 
     def hb_step(i, _):
@@ -684,8 +795,6 @@
         vgh[0:1, cols] = jnp.sum(hgrad[:, cols].astype(F32), axis=0, keepdims=True)
         return 0
     lax.fori_loop(0, F // TN, hb_step, 0)
-    dw_send(S, 3) if Z > 3 else None
-
     mgrad, jgrad, wo = b.mgrad, b.jgrad, b.w[O]
 
     def mixed_back(g):
@@ -720,8 +829,7 @@
             jgrad[rows, pl.ds(DT + a * AW, AW)] = (ak * scale).astype(BF)
             jgrad[rows, pl.ds(2 * DT + a * AW, AW)] = av.astype(BF)
 
-    rs_wait(1, 2)
-    obuf = b.obuf
+    obuf = n2.at[tc]
 
     def out_step(i, _):
         rows = ds(i * RB, RB, RB)
@@ -729,42 +837,48 @@
         v = (first[rows, :] + rs_value(1, rows) + vf[7:8, :]) * live_of(own_ends, r0, RB)
         obuf[rows, :] = v.astype(BF)
         return 0
+    def attb_step(g, _):
+        attend_back(g)
+        return 0
+
+    send(E, 0)
+    mixed_back(t)
+    tp_core(proj, b.tproj)
+    mixed_back(tc)
+    attend_back(t)
+    send(E, 1)
+    tp_x(proj, b.tproj)
+    attend_back(tc)
+    if X == 2:
+        mixed_back(tx)
+        attend_back(tx)
+    tp_last(proj, b.tproj)
+    for zz in range(ZT):
+        dw_compute(O, zz, lambda c0: mixed[:, ds(c0, 256, 256)],
+                   lambda cols: proj[:, :, cols].reshape(RT, 256))
+    if X == 2:
+        mixed_back(txc)
+        attend_back(txc)
+    send(E, 2)
+    for k in zorder:
+        dw_compute(J, k, lambda c0: n1[:, ds(c0, 256, 256)], lambda cols: jgrad[:, cols])
+    send(E, *range(3, Z))
+    dw_final(S)
+    rs_wait(1, 2)
     lax.fori_loop(0, nrb, out_step, 0)
     cp_out = pltpu.make_async_copy(obuf, o_out, loc.at[0])
     cp_out.start()
-
-    for g, arrive in order:
-        if arrive is not None:
-            arrive(proj, b.tproj)
-        mixed_back(g)
-
-    for zz in range(ZT):
-        dw_compute(O, zz, lambda c0: mixed[:, ds(c0, 256, 256)],
-                   lambda cols: proj[:, :, cols].reshape(RT, 256))
-
-    def attb_step(g, _):
-        attend_back(g)
-        return 0
-    lax.fori_loop(0, T // 2, attb_step, 0)
-    dw_send(S, 0)
-    dw_send(E, 1)
-    lax.fori_loop(T // 2, T, attb_step, 0)
-    dw_send(E, 2) if Z > 2 else None
-
-    for k in list(range(1, Z)) + [0]:
-        dw_compute(J, k, lambda c0: n1[:, ds(c0, 256, 256)], lambda cols: jgrad[:, cols])
     rs_start(0, 3, jgrad, wj, True)
-    dw_send(E, 3) if Z > 3 else None
-    dw_send(E, 0)
-    dw_final(S)
+    dwo_send()
+    send(J, 0)
     for i in range(2):
         j = 2 * i
         vg[2 + i:3 + i, ds(t * DT, DT, 128)] = jnp.sum(
             jgrad[:, pl.ds(j * DT, DT)].astype(F32), axis=0, keepdims=True)
-    dwo_send()
+    send(J, 1)
 
     rs_wait(0, 3)
-    tbuf = b.tbuf
+    tbuf = proj.at[tc]
 
     def ln1_back(i, carry):
         ag_, as_ = carry
@@ -793,9 +907,10 @@
             row = vgh[0:1, i * FB + r * Dn:i * FB + (r + 1) * Dn]
             for g in range(T):
                 v3[i, 8 + g * kk + r:9 + g * kk + r, :] = jnp.where(t == g, row, jnp.zeros_like(row))
-    vt = [rc(v3, v3c.at[0], b.svt[0].at[0], b.svt[1].at[0], core)]
-    vt[0].start()
-    vt[0].wait()
+    vt = rc(v3, v3c.at[0], b.svt[0].at[0], b.svt[1].at[0], core)
+    vt.start()
+    send(J, 2)
+    vt.wait()
     v3[...] = v3[...] + v3c[0]
     if X == 2:
         vx = rc(v3, v3c.at[1], b.svt[0].at[1], b.svt[1].at[1], xpeer)
@@ -811,11 +926,26 @@
         for m in range(1, Y):
             go(vy(m, k))
 
-    dw_send(J, 1)
+    dw_final(E)
+    copies = []
+
+    def emit(w, g):
+        for cp in out_copies(w, g):
+            cp.start()
+            copies.append(cp)
+
+    emit(S, t)
+    tp_core(b.fin[S], b.tfin[S])
+    emit(S, tc)
+    tp_x(b.fin[S], b.tfin[S])
+    if X == 2:
+        emit(S, tx)
+    send(J, *range(3, Z))
+
 
     def vz(k):
         return rc(v3s.at[k], v3z.at[k - 1], b.svz[0].at[k - 1], b.svz[1].at[k - 1], zpeer[k])
-    for k in list(range(1, Z)) + [0]:
+    for k in zorder:
         v = v3[zid[k] * Y + y]
         for m in range(1, Y):
             vy(m, k).wait_recv()
@@ -824,32 +954,19 @@
         if k:
             go(vz(k))
 
-    for k in range(2, Z):
-        dw_send(J, k)
-    dw_send(J, 0)
-
-    copies = []
-
-    def emit(w, g):
-        for cp in out_copies(w, g):
-            cp.start()
-            copies.append(cp)
-
-    dw_final(E)
+    emit(E, t)
+    tp_core(b.fin[E], b.tfin[E])
+    emit(E, tc)
+    tp_x(b.fin[E], b.tfin[E])
+    if X == 2:
+        emit(E, tx)
+    dw_final(J)
 
     @pl.when(mine)
     def _():
         dw_final(O)
         for i, dev in enumerate(peers):
             rc(b.fin[O].at[0], b.fin[O].at[0], b.tfo[0].at[i], b.tfo[1].at[0], dev).start()
-
-    for w in (S, E):
-        emit(w, t)
-        tp_core(b.fin[w], b.tfin[w])
-        emit(w, tc)
-        tp_x(b.fin[w], b.tfin[w])
-        if X == 2:
-            emit(w, tx)
 
     v = v3s[0]
     for k in range(1, Z):
@@ -859,29 +976,27 @@
     cp_v = pltpu.make_async_copy(b.vout, o_vec, loc.at[2])
     cp_v.start()
 
-    dw_final(J)
-    for w in (S, E):
+    emit(J, t)
+    tp_core(b.fin[J], b.tfin[J])
+    emit(J, tc)
+    tp_x(b.fin[J], b.tfin[J])
+    for w in (S, E, J):
         tp_last(b.fin[w], b.tfin[w])
         if X == 2:
             emit(w, txc)
+    if X == 2:
+        emit(J, tx)
 
     @pl.when(jnp.logical_not(mine))
     def _():
         rc(b.fin[O].at[0], b.fin[O].at[0], b.tfo[0].at[0], b.tfo[1].at[0], core).wait_recv()
     cp_o = pltpu.make_async_copy(b.fin[O].at[0], o_o, loc.at[3])
     cp_o.start()
-    w = J
-    emit(w, t)
-    tp_core(b.fin[w], b.tfin[w])
-    emit(w, tc)
-    tp_x(b.fin[w], b.tfin[w])
-    tp_last(b.fin[w], b.tfin[w])
-    if X == 2:
-        emit(w, tx)
-        emit(w, txc)
 
     for cp in pending:
         cp.wait_send()
+    for pred, cp in pending_if:
+        pl.when(pred)(cp.wait_send)
     for u, r in ((1, 2), (0, 3)):
         rs_done(u, r)
     wo_drain()

time: 234 us -> 202 us (0.86); the launches traced: 231 us -> 202 us
  Pallas kernels: 231 us -> 201 us
    pallas_call x1, Pallas kernels: 225 us -> 195 us  [body(): pl.pallas_call(functools.partial(kernel, q, tree), out_shape=(sds((R, D),...]
where the time goes in v2:
time: 202 us
  Pallas kernels  201 us (100%)
    pallas_call x1, Pallas kernels, body(): pl.pallas_call(functools.partial(kernel, q, tree), out_shape=(sds((R, D),...  195 us
    pallas_call x1, Pallas kernels, body(): pl.pallas_call(functools.partial(finish, divisor, q), grid=(steps,), out_...  5.72 us

profile of v2, /device:TPU:3, one launch (start us, length us, event | category | flops | bytes accessed | tf_op | source)
XLA Modules:
  0.0 201.8 jit_solution(14129516523174716768)
XLA Ops:
  0.7 195.2 %layer.1 = (bf16[256,1024]{1,0:T(8,128)(2,1)}, bf16[256,1024]{1,0:T(8,128)(2,1)}, f32[16,128]{1,0:T(8,128)}, bf16[128,3072]{1,0:T(8,128)(2,1)}, bf16[128,1024]{1...) custom-call(bf16[256,1024]{1,0:T(8,128)(2,1)} %refs_0_.1, s32[1,4]{1,0:T(1,128)} %refs_1_.1, ...), custom_call_target="tpu_custom_call" | custom-call | tf_op jit(solution)/shard_map/layer/pallas_call | solution.py:1038
  195.9 5.7 %finish.1 = (bf16[256,1024]{1,0:T(8,128)(2,1)}, bf16[256,1024]{1,0:T(8,128)(2,1)}, f32[128,3072]{1,0:T(8,128)}, f32[128,1024]{1,0:T(8,128)}, f32[128,4096]{1,0:T...) custom-call(bf16[256,1024]{1,0:T(8,128)(2,1)} %get-tuple-element.37., ...), custom_call_target="tpu_custom_call" | custom-call | tf_op jit(solution)/shard_map/finish/pallas_call | solution.py:1063

commit v3 on v2

--- a/solution.py
+++ b/solution.py
@@ -36,6 +36,7 @@
         self.F = hidden // T
         self.FB = hidden // n_fsdp // T
         self.ZT = self.Z // T
+        self.OS = 2 if self.ZT <= 2 else 2 + self.ZT
 
 
 def dot_nn(a, b):
@@ -101,11 +102,11 @@
     m.rs = [[DMA((q.X,)), DMA((q.X,)), DMA((1,)), DMA((1,))] for _ in range(4)]
     m.dw = [V((bz, q.Y * rb, C), BF) for bz, rb, C in q.grads]
     m.yr = [V((q.Y - 1, bz, rb, C), BF) for bz, rb, C in q.grads]
-    m.zr = [V((q.Z - 1, rb, C), BF) for bz, rb, C in q.grads]
+    m.zr = [V((q.OS if w == O else q.Z - 1, rb, C), BF) for w, (bz, rb, C) in enumerate(q.grads)]
     m.zq = [V((16, 128) if w == O else (rb, C), BF) for w, (bz, rb, C) in enumerate(q.grads)]
     m.fin = [V((1 if w == O else T, rb, C), BF) for w, (bz, rb, C) in enumerate(q.grads)]
     m.sy = [[DMA((q.Y - 1, bz)), DMA((q.Y - 1, bz))] for bz, rb, C in q.grads]
-    m.sz = [[DMA((q.Z - 1,)), DMA((q.Z,))] for _ in q.grads]
+    m.sz = [[DMA((max(q.Z - 1, q.ZT),)), DMA((max(q.Z, q.OS),))] for _ in q.grads]
     m.sout = [DMA((T, q.n)) for _ in q.grads]
     m.gz = [[DMA((q.Z,)), DMA((max(q.Z - 1, q.ZT),))] for _ in range(5)]
     m.gy = [[DMA((q.Y - 1, q.Z)), DMA((q.Y - 1, q.Z))] for _ in range(5)]
@@ -337,10 +338,12 @@
     fw(J, 0)
     cp_tok.wait()
     tp_send(b.tok, b.ttok)
-    wo_z()
     last = range(4, max(Z, 5))
 
     fw(VEC, *range(1, Z))
+    for cp in cp_e:
+        cp.wait()
+    fw(E, 0)
     ag_wait(VEC)
     vf, hb = b.vf, b.hb
     for i in range(n):
@@ -374,6 +377,7 @@
         places = lax.broadcasted_iota(jnp.int32, (rows, 1), 0) + r0
         return (places < ends[-1]).astype(F32)
 
+    fw(J, 1)
     own_ends = ends_of(t)
     cp_cot.wait()
     cot = b.cot
@@ -398,23 +402,20 @@
         lax.fori_loop(0, nrb, step, 0)
 
     ln1(t)
+    fw(J, 2)
     tp_core(tok, b.ttok)
     ln1(tc)
-    fw(J, 1)
+    wo_z()
+    fw(J, 3)
     tp_x(tok, b.ttok)
-    fw(J, 2)
     if X == 2:
         ln1(tx)
+    fw(J, *last)
+    if X == 2:
         tp_last(tok, b.ttok)
         ln1(txc)
-    fw(J, 3)
-    fw(J, *last)
-    for cp in cp_e:
-        cp.wait()
+    ag_wait(J)
     ag_z(E)
-    fw(E, 0)
-    ag_wait(J)
-
     qkv, wj = b.qkv, b.w[J]
     TN = 256
     for j in range(3):
@@ -427,6 +428,7 @@
             return 0
         lax.fori_loop(0, DT // TN, step, 0)
 
+    wo_y()
     scale = hd ** (-0.5)
     prob, mixed = b.prob, b.mixed
     AW = 256
@@ -470,7 +472,6 @@
         return 0
 
     lax.fori_loop(0, T, att_step, 0)
-    wo_y()
     cp_shr.wait()
     ag_z(S)
     fw(E, 1)
@@ -492,7 +493,7 @@
     def rs_xcopy(u, r):
         return rc(b.xsend[u], b.xrecv[u], b.rs[r][2].at[0], b.rs[r][3].at[0], xpeer)
 
-    def rs_start(u, r, lhs, rhs, nt):
+    def rs_start(u, r, lhs, rhs, nt, put_own=None):
         ps = b.psend[u]
 
         def put_at(i):
@@ -518,15 +519,17 @@
             rs_xcopy(u, r).start()
         block_mm(lhs, tc, rhs, nt, put_at(0))
         rs_copy(u, r, 0).start()
-        block_mm(lhs, t, rhs, nt, put_acc)
+        block_mm(lhs, t, rhs, nt, put_own or put_acc)
 
     def rs_wait(u, r):
         rs_copy(u, r, 0).wait_recv()
         if X == 2:
             rs_xcopy(u, r).wait_recv()
 
-    def rs_value(u, rows):
-        v = acc0[rows, :] + b.precv[u][0, rows, :].astype(F32)
+    def rs_value(u, rows, own=True):
+        v = b.precv[u][0, rows, :].astype(F32)
+        if own:
+            v = acc0[rows, :] + v
         if X == 2:
             v = v + b.xrecv[u][rows, :].astype(F32)
         return v
@@ -542,6 +545,8 @@
     tp_x(cot, b.tcot)
     fw(E, 2)
     fw(E, 3)
+    fw(S, 0)
+    fw(E, *last)
     rs_wait(0, 0)
     first, n2 = b.first, b.n2
 
@@ -554,10 +559,9 @@
         return 0
     lax.fori_loop(0, nrb, ln2, 0)
     tp_send(n2, b.tn2)
-    fw(E, *last)
-    fw(S, 0)
     rs_done(0, 0)
     tp_last(cot, b.tcot)
+    fw(S, 1)
     ag_wait(E)
 
     hact, dgelu, we, ws = b.hact, b.dgelu, b.w[E], b.w[S]
@@ -576,14 +580,13 @@
     up(t)
     tp_core(n2, b.tn2)
     up(tc)
-    fw(S, 1)
+    fw(S, 2)
+    fw(S, 3)
     tp_x(n2, b.tn2)
     if X == 2:
         up(tx)
         tp_last(n2, b.tn2)
         up(txc)
-    fw(S, 2)
-    fw(S, 3)
     fw(S, *last)
 
     def blocks(w):
@@ -637,9 +640,12 @@
         return rc(b.dw[w].at[zid[k], ds(y * rb, rb, 16)], b.zr[w].at[k - 1],
                   b.sz[w][0].at[k - 1], b.sz[w][1].at[k - 1], zpeer[k])
 
-    def dw_o(zz, k):
-        return rc(b.dw[O].at[zz, ds(y * Dn, Dn, 16)], b.zr[O].at[k - 1],
-                  b.sz[O][0].at[k - 1], b.sz[O][1].at[k - 1], zpeer[k])
+    def dw_o(zz, i, to):
+        return rc(b.dw[O].at[zz, ds(y * Dn, Dn, 16)], b.zr[O].at[i], b.sz[O][0].at[zz],
+                  b.sz[O][1].at[i], (dp, to * Y + y))
+
+    def relay_slot(zz):
+        return zz if ZT <= 2 else 2 + zz
 
     def dw_relay(w):
         rb = blocks(w)[1]
@@ -667,17 +673,35 @@
         if k:
             go(dw_z(w, k))
 
-    def dwo_send(drain=False):
+    def dwo_hops(act_near, act_far):
         for zz in range(ZT):
-            if not drain:
-                dw_sum(O, zz)
-            for k in range(1, Z):
-                @pl.when(zid[k] == zlo + zz)
-                def _(zz=zz, k=k):
-                    if drain:
-                        dw_o(zz, k).wait_send()
-                    else:
-                        dw_o(zz, k).start()
+            zo = zlo + zz
+            far = z // 2 != zo // 2
+            near = jnp.logical_and(z // 2 == zo // 2, z != zo)
+            if Z > 1:
+                pl.when(near)(lambda zz=zz, zo=zo: act_near(dw_o(zz, 0, zo)))
+            if Z > 2:
+                pl.when(jnp.logical_and(far, outer))(lambda zz=zz: act_near(dw_o(zz, relay_slot(zz), zid[1])))
+                pl.when(jnp.logical_and(far, inner))(lambda zz=zz, zo=zo: act_far(zz, dw_o(zz, 1, zo)))
+
+    def dwo_first():
+        for zz in range(ZT):
+            dw_sum(O, zz)
+        dwo_hops(lambda cp: cp.start(), lambda zz, cp: None)
+
+    def dwo_second():
+        def pass_on(zz, cp):
+            dw_o(zz, relay_slot(zz), z).wait_recv()
+            ch = 64
+
+            def add(j, _):
+                rows = ds(y * Dn + j * ch, ch, 64)
+                v = b.dw[O][zz, rows, :].astype(F32) + b.zr[O][relay_slot(zz), ds(j * ch, ch, 64), :].astype(F32)
+                b.dw[O][zz, rows, :] = v.astype(BF)
+                return 0
+            lax.fori_loop(0, Dn // ch, add, 0)
+            cp.start()
+        dwo_hops(lambda cp: None, pass_on)
 
     def dw_final(w):
         bz, rb, C = blocks(w)
@@ -686,24 +710,31 @@
         own = z - zlo if w == O else z
         me = 0 if w == O else t
 
-        def total(ks):
-            for k in ks:
-                (dw_o(0, k) if w == O else dw_z(w, k)).wait_recv()
-
+        def total(slots):
             def add(i, _):
                 rows = ds(i * ch, ch, 64)
                 v = b.dw[w][own, ds(y * rb + i * ch, ch, 64), :].astype(F32)
-                for k in ks:
-                    v = v + b.zr[w][k - 1, rows, :].astype(F32)
+                for i_slot in slots:
+                    v = v + b.zr[w][i_slot, rows, :].astype(F32)
                 fin[me, rows, :] = v.astype(BF)
                 return 0
             lax.fori_loop(0, rb // ch, add, 0)
 
-        if relay and w != O:
-            pl.when(inner)(lambda: total((1, 2, 3)))
-            pl.when(outer)(lambda: total((1, 2)))
+        def wait_total(ks):
+            for k in ks:
+                dw_z(w, k).wait_recv()
+            total([k - 1 for k in ks])
+
+        if w == O:
+            ends = range(min(Z - 1, 2))
+            for i in ends:
+                dw_o(own, i, z).wait_recv()
+            total(ends)
+        elif relay:
+            pl.when(inner)(lambda: wait_total((1, 2, 3)))
+            pl.when(outer)(lambda: wait_total((1, 2)))
         else:
-            total(range(1, Z))
+            wait_total(range(1, Z))
         if w != O:
             tp_send(fin, b.tfin[w])
 
@@ -720,7 +751,7 @@
     def cot_rhs(cols):
         return cot[:, :, cols].reshape(RT, 256)
 
-    zorder = ([3, 1, 2] if relay else list(range(1, Z))) + [0]
+    zorder = ([3, 2, 1] if relay else list(range(1, Z))) + [0]
     half = len(zorder) // 2
 
     def dw_shrink(ks):
@@ -788,7 +819,10 @@
     rs_done(0, 1)
 
     send(S, *range(3, Z))
-    rs_start(1, 2, hact, ws, False)
+    def add_to_first(cols, v):
+        first[:, cols] = first[:, cols] + v
+
+    rs_start(1, 2, hact, ws, False, add_to_first)
 
     def hb_step(i, _):
         cols = ds(i * TN, TN, 256)
@@ -834,7 +868,7 @@
     def out_step(i, _):
         rows = ds(i * RB, RB, RB)
         r0 = i * RB
-        v = (first[rows, :] + rs_value(1, rows) + vf[7:8, :]) * live_of(own_ends, r0, RB)
+        v = (first[rows, :] + rs_value(1, rows, False) + vf[7:8, :]) * live_of(own_ends, r0, RB)
         obuf[rows, :] = v.astype(BF)
         return 0
     def attb_step(g, _):
@@ -846,13 +880,14 @@
     tp_core(proj, b.tproj)
     mixed_back(tc)
     attend_back(t)
-    send(E, 1)
     tp_x(proj, b.tproj)
     attend_back(tc)
     if X == 2:
         mixed_back(tx)
         attend_back(tx)
+    send(E, 1)
     tp_last(proj, b.tproj)
+    dw_final(S)
     for zz in range(ZT):
         dw_compute(O, zz, lambda c0: mixed[:, ds(c0, 256, 256)],
                    lambda cols: proj[:, :, cols].reshape(RT, 256))
@@ -860,23 +895,24 @@
         mixed_back(txc)
         attend_back(txc)
     send(E, 2)
+    rs_start(0, 3, jgrad, wj, True)
     for k in zorder:
         dw_compute(J, k, lambda c0: n1[:, ds(c0, 256, 256)], lambda cols: jgrad[:, cols])
+    dwo_first()
     send(E, *range(3, Z))
-    dw_final(S)
+    dw_final(E)
     rs_wait(1, 2)
     lax.fori_loop(0, nrb, out_step, 0)
     cp_out = pltpu.make_async_copy(obuf, o_out, loc.at[0])
     cp_out.start()
-    rs_start(0, 3, jgrad, wj, True)
-    dwo_send()
-    send(J, 0)
     for i in range(2):
         j = 2 * i
         vg[2 + i:3 + i, ds(t * DT, DT, 128)] = jnp.sum(
             jgrad[:, pl.ds(j * DT, DT)].astype(F32), axis=0, keepdims=True)
+    send(J, 0)
+    dwo_second()
     send(J, 1)
-
+    send(J, 2)
     rs_wait(0, 3)
     tbuf = proj.at[tc]
 
@@ -909,12 +945,24 @@
                 v3[i, 8 + g * kk + r:9 + g * kk + r, :] = jnp.where(t == g, row, jnp.zeros_like(row))
     vt = rc(v3, v3c.at[0], b.svt[0].at[0], b.svt[1].at[0], core)
     vt.start()
-    send(J, 2)
+    send(J, *range(3, Z))
     vt.wait()
     v3[...] = v3[...] + v3c[0]
     if X == 2:
         vx = rc(v3, v3c.at[1], b.svt[0].at[1], b.svt[1].at[1], xpeer)
         vx.start()
+    owner = z // ZT
+
+    def fo_copy(i, dev):
+        return rc(b.fin[O].at[0], b.fin[O].at[0], b.tfo[0].at[i], b.tfo[1].at[0], dev)
+
+    @pl.when(mine)
+    def _():
+        dw_final(O)
+        fo_copy(0, core).start()
+        if X == 2:
+            fo_copy(1, xpeer).start()
+    if X == 2:
         vx.wait()
         v3[...] = v3[...] + v3c[1]
     v3y, v3s, v3z = b.v3y, b.v3s, b.v3z
@@ -926,7 +974,6 @@
         for m in range(1, Y):
             go(vy(m, k))
 
-    dw_final(E)
     copies = []
 
     def emit(w, g):
@@ -940,8 +987,7 @@
     tp_x(b.fin[S], b.tfin[S])
     if X == 2:
         emit(S, tx)
-    send(J, *range(3, Z))
-
+    dw_final(J)
 
     def vz(k):
         return rc(v3s.at[k], v3z.at[k - 1], b.svz[0].at[k - 1], b.svz[1].at[k - 1], zpeer[k])
@@ -954,19 +1000,19 @@
         if k:
             go(vz(k))
 
+    @pl.when(jnp.logical_not(mine))
+    def _():
+        fo_copy(0, core).wait_recv()
+    if X == 2:
+        pl.when(tx == owner)(lambda: fo_copy(2, core).start())
+    cp_o = pltpu.make_async_copy(b.fin[O].at[0], o_o, loc.at[3])
+    cp_o.start()
     emit(E, t)
     tp_core(b.fin[E], b.tfin[E])
     emit(E, tc)
     tp_x(b.fin[E], b.tfin[E])
     if X == 2:
         emit(E, tx)
-    dw_final(J)
-
-    @pl.when(mine)
-    def _():
-        dw_final(O)
-        for i, dev in enumerate(peers):
-            rc(b.fin[O].at[0], b.fin[O].at[0], b.tfo[0].at[i], b.tfo[1].at[0], dev).start()
 
     v = v3s[0]
     for k in range(1, Z):
@@ -987,12 +1033,6 @@
     if X == 2:
         emit(J, tx)
 
-    @pl.when(jnp.logical_not(mine))
-    def _():
-        rc(b.fin[O].at[0], b.fin[O].at[0], b.tfo[0].at[0], b.tfo[1].at[0], core).wait_recv()
-    cp_o = pltpu.make_async_copy(b.fin[O].at[0], o_o, loc.at[3])
-    cp_o.start()
-
     for cp in pending:
         cp.wait_send()
     for pred, cp in pending_if:
@@ -1000,12 +1040,15 @@
     for u, r in ((1, 2), (0, 3)):
         rs_done(u, r)
     wo_drain()
-    dwo_send(drain=True)
+    dwo_hops(lambda cp: cp.wait_send(), lambda zz, cp: cp.wait_send())
 
     @pl.when(mine)
     def _():
-        for i, dev in enumerate(peers):
-            rc(b.fin[O].at[0], b.fin[O].at[0], b.tfo[0].at[i], b.tfo[1].at[0], dev).wait_send()
+        fo_copy(0, core).wait_send()
+        if X == 2:
+            fo_copy(1, xpeer).wait_send()
+    if X == 2:
+        pl.when(tx == owner)(lambda: fo_copy(2, core).wait_send())
     for cp in copies + [cp_out, cp_tg, cp_v, cp_o]:
         cp.wait()
 

time: 202 us -> 182 us (0.901)
  Pallas kernels: 201 us -> 181 us
    pallas_call x1, Pallas kernels: 195 us -> 176 us  [body(): pl.pallas_call(functools.partial(kernel, q, tree), out_shape=(sds((R, D),...]
where the time goes in v3:
time: 182 us
  Pallas kernels  181 us (99%)
    pallas_call x1, Pallas kernels, body(): pl.pallas_call(functools.partial(kernel, q, tree), out_shape=(sds((R, D),...  176 us
    pallas_call x1, Pallas kernels, body(): pl.pallas_call(functools.partial(finish, divisor, q), grid=(steps,), out_...  5.72 us

profile of v3, /device:TPU:3, one launch (start us, length us, event | category | flops | bytes accessed | tf_op | source)
XLA Modules:
  0.0 182.2 jit_solution(5396832553626867666)
XLA Ops:
  0.7 175.7 %layer.1 = (bf16[256,1024]{1,0:T(8,128)(2,1)}, bf16[256,1024]{1,0:T(8,128)(2,1)}, f32[16,128]{1,0:T(8,128)}, bf16[128,3072]{1,0:T(8,128)(2,1)}, bf16[128,1024]{1...) custom-call(bf16[256,1024]{1,0:T(8,128)(2,1)} %refs_0_.1, s32[1,4]{1,0:T(1,128)} %refs_1_.1, ...), custom_call_target="tpu_custom_call" | custom-call | tf_op jit(solution)/shard_map/layer/pallas_call | solution.py:1081
  176.3 5.7 %finish.1 = (bf16[256,1024]{1,0:T(8,128)(2,1)}, bf16[256,1024]{1,0:T(8,128)(2,1)}, f32[128,3072]{1,0:T(8,128)}, f32[128,1024]{1,0:T(8,128)}, f32[128,4096]{1,0:T...) custom-call(bf16[256,1024]{1,0:T(8,128)(2,1)} %get-tuple-element.37., ...), custom_call_target="tpu_custom_call" | custom-call | tf_op jit(solution)/shard_map/finish/pallas_call | solution.py:1106

commit v4 on v3

--- a/solution.py
+++ b/solution.py
@@ -110,6 +110,8 @@
     m.sout = [DMA((T, q.n)) for _ in q.grads]
     m.gz = [[DMA((q.Z,)), DMA((max(q.Z - 1, q.ZT),))] for _ in range(5)]
     m.gy = [[DMA((q.Y - 1, q.Z)), DMA((q.Y - 1, q.Z))] for _ in range(5)]
+    m.hy = [DMA((q.Y - 1,)), DMA((q.Y - 1,))]
+    m.hz = [DMA((q.Y, q.Z)), DMA((q.Y, max(q.Z - 1, 1)))]
     pair = lambda: [DMA((3,)), DMA((3,))]
     m.ttok, m.tcot, m.tn2, m.tproj, m.tcnt, m.tfo = (pair() for _ in range(6))
     m.tfin = [pair() for _ in q.grads]
@@ -209,7 +211,7 @@
         if w == VEC:
             return b.vec.at[src_s]
         if w == S:
-            return b.w[S].at[ds(src_s * FB, FB, 16)]
+            return b.w[S].at[ds(src_s * FB, FB // 2, 16)]
         return b.w[w].at[ds(src_s * Dn, Dn, 16)]
 
     def gz_copy(w, k):
@@ -267,6 +269,44 @@
             for m in range(1, Y):
                 src = zid[k] * Y + ysrc[m]
                 rc(slot(w, src), slot(w, src), b.gy[w][0].at[m - 1, k], b.gy[w][1].at[m - 1, k], ypeer[m]).wait_recv()
+
+    def hslot(zz, yy):
+        return b.w[S].at[ds((zz * Y + yy) * FB + FB // 2, FB // 2, 16)]
+
+    def half_y(m, src):
+        return rc(hslot(z, src), hslot(z, src), b.hy[0].at[m - 1], b.hy[1].at[m - 1], ypeer[m])
+
+    def half_z(m, k, zz):
+        piece = hslot(zz, ysrc[m])
+        return rc(piece, piece, b.hz[0].at[m, k - 1], b.hz[1].at[m, k - 1], zpeer[k])
+
+    def half_start():
+        for m in range(1, Y):
+            go(half_y(m, y))
+
+    def half_send(*ms):
+        for m in ms:
+            if m:
+                half_y(m, ysrc[m]).wait_recv()
+            for k in ([1, 3, 2] if relay else range(1, Z)):
+                if relay and k == 3:
+                    go_if(inner, half_z(m, k, z))
+                else:
+                    go(half_z(m, k, z))
+
+    def half_relay(m):
+        if relay:
+            pl.when(inner)(lambda: half_z(m, 2, zid[2]).wait_recv())
+            piece = hslot(zid[2], ysrc[m])
+            go_if(inner, rc(piece, piece, b.hz[0].at[m, Z - 1], b.hz[1].at[m, 2], (dp, zfar * Y + y)))
+
+    def half_wait():
+        for m in range(Y):
+            for k in range(1, Z):
+                if relay and k == 2:
+                    pl.when(outer)(lambda m=m: half_z(m, 2, zid[2]).wait_recv())
+                else:
+                    half_z(m, k, zid[k]).wait_recv()
 
     zlo = t * ZT
     mine = z // ZT == t
@@ -474,6 +514,7 @@
     lax.fori_loop(0, T, att_step, 0)
     cp_shr.wait()
     ag_z(S)
+    half_send(0)
     fw(E, 1)
     wo_wait()
 
@@ -545,6 +586,7 @@
     tp_x(cot, b.tcot)
     fw(E, 2)
     fw(E, 3)
+    half_start()
     fw(S, 0)
     fw(E, *last)
     rs_wait(0, 0)
@@ -561,6 +603,7 @@
     tp_send(n2, b.tn2)
     rs_done(0, 0)
     tp_last(cot, b.tcot)
+    half_send(*range(1, Y))
     fw(S, 1)
     ag_wait(E)
 
@@ -582,6 +625,7 @@
     up(tc)
     fw(S, 2)
     fw(S, 3)
+    half_relay(0)
     tp_x(n2, b.tn2)
     if X == 2:
         up(tx)
@@ -607,7 +651,7 @@
         bz, rb, C = blocks(w)
         sl = dw_slot(w, k)
         tile = Y * rb
-        TC = 256
+        TC = next(v for v in (512, 768, 256) if C % v == 0)
 
         def step(i, _):
             cols = ds(i * TC, TC, 256)
@@ -749,7 +793,7 @@
         return [pltpu.make_async_copy(fin.at[g], o_s.at[ds(g * FB, FB, 16)], so.at[g, 0])]
 
     def cot_rhs(cols):
-        return cot[:, :, cols].reshape(RT, 256)
+        return cot[:, :, cols].reshape(RT, cols.size)
 
     zorder = ([3, 2, 1] if relay else list(range(1, Z))) + [0]
     half = len(zorder) // 2
@@ -759,29 +803,27 @@
             dw_compute(S, k, lambda c0: hact[:, ds(c0, 256, 256)], cot_rhs)
 
     dw_shrink(zorder[:half])
+    for m in range(1, Y):
+        half_relay(m)
     dw_shrink(zorder[half:])
     ag_wait(S)
+    half_wait()
     hgrad = b.hgrad
 
-    def down(g, acc):
-        def step(i, _):
-            cols = ds(i * TN, TN, 256)
-            rows = ds(g * R, R, 256)
-            v = dot_nt(cot[g], ws[cols, :]) * dgelu[rows, cols].astype(F32)
-            hgrad[rows, cols] = v.astype(BF)
-            return 0
-        lax.fori_loop(0, F // TN, step, 0)
-        return acc
-
-    lax.fori_loop(0, T, down, 0)
+    def down(i, _):
+        cols = ds(i * TN, TN, 256)
+        v = dot_nt(cot[...].reshape(RT, D), ws[cols, :]) * dgelu[:, cols].astype(F32)
+        hgrad[:, cols] = v.astype(BF)
+        return 0
+
+    lax.fori_loop(0, F // TN, down, 0)
     def send(w, *steps):
         for i in steps:
             if i < Z:
                 dw_send(w, zorder[i])
 
+    rs_start(0, 1, hgrad, we, True)
     send(S, 0)
-    rs_start(0, 1, hgrad, we, True)
-    send(S, 1)
 
     def dw_expand(ks):
         for k in ks:
@@ -789,8 +831,9 @@
                        lambda cols: hgrad[:, cols])
 
     dw_expand(zorder[:half])
+    send(S, 1)
+    dw_expand(zorder[half:])
     send(S, 2)
-    dw_expand(zorder[half:])
     rs_wait(0, 1)
     proj, fgrad = b.proj, b.fgrad
 
@@ -890,7 +933,7 @@
     dw_final(S)
     for zz in range(ZT):
         dw_compute(O, zz, lambda c0: mixed[:, ds(c0, 256, 256)],
-                   lambda cols: proj[:, :, cols].reshape(RT, 256))
+                   lambda cols: proj[:, :, cols].reshape(RT, cols.size))
     if X == 2:
         mixed_back(txc)
         attend_back(txc)

time: 182 us -> 176 us (0.967)
  Pallas kernels: 181 us -> 175 us
    pallas_call x1, Pallas kernels: 176 us -> 169 us  [body(): pl.pallas_call(functools.partial(kernel, q, tree), out_shape=(sds((R, D),...]
where the time goes in v4:
time: 176 us
  Pallas kernels  175 us (99%)
    pallas_call x1, Pallas kernels, body(): pl.pallas_call(functools.partial(kernel, q, tree), out_shape=(sds((R, D),...  169 us
    pallas_call x1, Pallas kernels, body(): pl.pallas_call(functools.partial(finish, divisor, q), grid=(steps,), out_...  5.72 us

profile of v4, /device:TPU:3, one launch (start us, length us, event | category | flops | bytes accessed | tf_op | source)
XLA Modules:
  0.0 175.7 jit_solution(2043389189890611279)
XLA Ops:
  0.7 169.2 %layer.1 = (bf16[256,1024]{1,0:T(8,128)(2,1)}, bf16[256,1024]{1,0:T(8,128)(2,1)}, f32[16,128]{1,0:T(8,128)}, bf16[128,3072]{1,0:T(8,128)(2,1)}, bf16[128,1024]{1...) custom-call(bf16[256,1024]{1,0:T(8,128)(2,1)} %refs_0_.1, s32[1,4]{1,0:T(1,128)} %refs_1_.1, ...), custom_call_target="tpu_custom_call" | custom-call | tf_op jit(solution)/shard_map/layer/pallas_call | solution.py:1124
  169.9 5.7 %finish.1 = (bf16[256,1024]{1,0:T(8,128)(2,1)}, bf16[256,1024]{1,0:T(8,128)(2,1)}, f32[128,3072]{1,0:T(8,128)}, f32[128,1024]{1,0:T(8,128)}, f32[128,4096]{1,0:T...) custom-call(bf16[256,1024]{1,0:T(8,128)(2,1)} %get-tuple-element.37., ...), custom_call_target="tpu_custom_call" | custom-call | tf_op jit(solution)/shard_map/finish/pallas_call | solution.py:1149
